TPU v7x, 128 devices: a whole 4x4x4 slice. The times are simulated.
128 devices in a mesh: ctx: 16 (over z_lo, x, core), tp: 8 (over y, z_hi).
Axes of the slice: x: 4, y: 4, z: 4 (z_hi: 2, z_lo: 2; z = z_hi * 2 + z_lo), core: 2. Of those that a mesh axis runs over, the one named last changes fastest.
Arguments:
- queries: bfloat16 [4096, 8192], P(('ctx', 'tp')), may hold values from -5.5 to 5.5
- keys: bfloat16 [4096, 1024], P(('ctx', 'tp')), may hold values from -5.5 to 5.5
- values: bfloat16 [4096, 1024], P(('ctx', 'tp')), may hold values from -6 to 6
- out_grad: bfloat16 [4096, 8192], P(('ctx', 'tp')), may hold values from -6 to 6
- doc_ids: int32 [4096], replicated, may hold values from 0 to 3, never falling along the last dimension, each value on 1 to 3840 neighbouring positions
Outputs:
- attended: float32 [4096, 8192], P(('ctx', 'tp'))
- query_grad: float32 [4096, 8192], P(('ctx', 'tp'))
- key_grad: float32 [4096, 1024], P(('ctx', 'tp'))
- value_grad: float32 [4096, 1024], P(('ctx', 'tp'))
Inputs may be any that keep to these rules, and one draw needn't show every extreme that they name: doc_ids never falls along the sequence; each document holds 3840 tokens or fewer, and one holds exactly 3840.
All inputs are finite; a program needn't handle non-finite values.
Results may differ from a plain program's by a relative error of at most 0.019.
Values may be sent and summed in bfloat16 or wider, within the bound.
No kernel may reach another device: no remote copies, remote signals or barrier semaphores. Data moves between devices by JAX's collectives and lax.ppermute only.
A program may use at most 64 MiB of HBM per device.

v0:
```python
import jax
import jax.numpy as jnp
from jax import lax
from jax.sharding import PartitionSpec as P

HD = 128


very_low = -1e30


def per_device(queries, keys, values, out_grad, doc_ids):
    queries_here, keys_here, values_here, grads_here = (
        lax.all_to_all(queries, "tp", split_axis=1, concat_axis=0, tiled=True),
        lax.all_to_all(keys, "tp", split_axis=1, concat_axis=0, tiled=True),
        lax.all_to_all(values, "tp", split_axis=1, concat_axis=0, tiled=True),
        lax.all_to_all(out_grad, "tp", split_axis=1, concat_axis=0, tiled=True),
    )
    shard_rows = queries_here.shape[0]
    kv_heads = keys_here.shape[1] // HD
    group_size = queries_here.shape[1] // (kv_heads * HD)
    score_scale = HD ** (-0.5)
    block = min(512, shard_rows)
    whole_len = doc_ids.shape[0]
    my_index = lax.axis_index("ctx")
    q_first = my_index * shard_rows
    q_last = q_first + shard_rows - 1
    q_pos = q_first + jnp.arange(shard_rows, dtype=jnp.int32)
    q_doc = lax.dynamic_slice_in_dim(doc_ids, q_first, shard_rows, 0)
    q_four = queries_here.reshape(shard_rows, kv_heads, group_size, HD)
    g_four = grads_here.reshape(shard_rows, kv_heads, group_size, HD)

    def active(kstart):
        last_key = jnp.clip(jnp.minimum(kstart + block - 1, q_last), 0, whole_len - 1)
        doc_last = lax.dynamic_index_in_dim(doc_ids, last_key, 0, keepdims=False)
        return (kstart >= 0) & (kstart <= q_last) & (doc_last >= q_doc[0])

    def scored(key_block, kstart):
        key_pos = kstart + jnp.arange(block, dtype=jnp.int32)
        key_doc = lax.dynamic_slice_in_dim(doc_ids, jnp.maximum(kstart, 0), block, 0)
        allowed = (key_pos[None, :] <= q_pos[:, None]) & (key_doc[None, :] == q_doc[:, None])
        scores = (
            jnp.einsum("ighd,jgd->ghij", q_four, key_block, preferred_element_type=jnp.float32)
            * score_scale
        )
        return (jnp.where(allowed, scores, very_low), allowed)

    stat_start = (
        jnp.full((kv_heads, group_size, shard_rows), very_low, jnp.float32),
        jnp.zeros((kv_heads, group_size, shard_rows), jnp.float32),
    )
    key_part = lax.all_gather(keys_here, "ctx", axis=0, tiled=True)
    block_count = key_part.shape[0] // block
    key_blocks = key_part.reshape(block_count, block, kv_heads, HD)

    def stats_advance(running, block_item):
        key_block, block_index = block_item
        kstart = block_index * block

        def stats_compute(running):
            row_max, row_sum = running
            scores, allowed = scored(key_block, kstart)
            new_max = jnp.maximum(row_max, jnp.max(scores, axis=-1))
            weights = jnp.where(allowed, jnp.exp(scores - new_max[..., None]), 0.0)
            row_sum = row_sum * jnp.exp(row_max - new_max) + jnp.sum(weights, axis=-1)
            return (new_max, row_sum)

        return (lax.cond(active(kstart), stats_compute, lambda unchanged: unchanged, running), None)

    running, _ = lax.scan(
        stats_advance, stat_start, (key_blocks, jnp.arange(block_count, dtype=jnp.int32))
    )
    row_max, row_sum = running
    log_total = row_max + jnp.log(row_sum)
    mix_start = jnp.zeros((kv_heads, group_size, shard_rows, HD), jnp.float32)
    weighted = mix_start
    key_part = lax.all_gather(keys_here, "ctx", axis=0, tiled=True)
    value_part = lax.all_gather(values_here, "ctx", axis=0, tiled=True)
    block_count = key_part.shape[0] // block
    key_blocks = key_part.reshape(block_count, block, kv_heads, HD)
    value_blocks = value_part.reshape(block_count, block, kv_heads, HD)

    def mix_advance(weighted, block_item):
        key_block, value_block, block_index = block_item
        kstart = block_index * block

        def mix_compute(weighted):
            scores, allowed = scored(key_block, kstart)
            attn_prob = jnp.where(allowed, jnp.exp(scores - log_total[..., None]), 0.0)
            return weighted + jnp.einsum(
                "ghij,jgd->ghid",
                attn_prob.astype(jnp.bfloat16),
                value_block,
                preferred_element_type=jnp.float32,
            )

        return (lax.cond(active(kstart), mix_compute, lambda unchanged: unchanged, weighted), None)

    weighted, _ = lax.scan(
        mix_advance, weighted, (key_blocks, value_blocks, jnp.arange(block_count, dtype=jnp.int32))
    )
    out_four = weighted.transpose(2, 0, 1, 3)
    row_delta = jnp.sum(g_four.astype(jnp.float32) * out_four, axis=-1).transpose(1, 2, 0)
    grad_start = jnp.zeros((shard_rows, kv_heads, group_size, HD), jnp.float32)
    grad_q = grad_start
    backward_grad_q = grad_q
    key_part = lax.all_gather(keys_here, "ctx", axis=0, tiled=True)
    value_part = lax.all_gather(values_here, "ctx", axis=0, tiled=True)
    block_count = key_part.shape[0] // block
    key_blocks = key_part.reshape(block_count, block, kv_heads, HD)
    value_blocks = value_part.reshape(block_count, block, kv_heads, HD)

    def backward_advance(grad_acc, block_item):
        key_block, value_block, block_index = block_item
        kstart = block_index * block

        def backward_compute(grad_acc):
            scores, allowed = scored(key_block, kstart)
            attn_prob = jnp.where(allowed, jnp.exp(scores - log_total[..., None]), 0.0)
            prob_half = attn_prob.astype(jnp.bfloat16)
            grad_v = jnp.einsum(
                "ghij,ighd->jgd", prob_half, g_four, preferred_element_type=jnp.float32
            )
            grad_prob = jnp.einsum(
                "ighd,jgd->ghij", g_four, value_block, preferred_element_type=jnp.float32
            )
            grad_score = (attn_prob * (grad_prob - row_delta[..., None])).astype(jnp.bfloat16)
            grad_acc = (
                grad_acc
                + jnp.einsum(
                    "ghij,jgd->ighd", grad_score, key_block, preferred_element_type=jnp.float32
                )
                * score_scale
            )
            grad_k = (
                jnp.einsum("ghij,ighd->jgd", grad_score, q_four, preferred_element_type=jnp.float32)
                * score_scale
            )
            return (grad_acc, grad_k, grad_v)

        def skipped(grad_acc):
            empty = jnp.zeros((block, kv_heads, HD), jnp.float32)
            return (grad_acc, empty, empty)

        grad_acc, grad_k, grad_v = lax.cond(active(kstart), backward_compute, skipped, grad_acc)
        kv_block = jnp.concatenate(
            [grad_k.reshape(block, kv_heads * HD), grad_v.reshape(block, kv_heads * HD)], 1
        )
        return (grad_acc, kv_block)

    backward_grad_q, kv_blocks = lax.scan(
        backward_advance,
        backward_grad_q,
        (key_blocks, value_blocks, jnp.arange(block_count, dtype=jnp.int32)),
    )
    grad_q = backward_grad_q
    kv_part = kv_blocks.reshape(block_count * block, 2 * kv_heads * HD)
    kv_buffer = kv_part
    grad_q, kv_buffer = (grad_q, kv_buffer)
    kv_grad = lax.psum_scatter(
        kv_buffer.astype(jnp.bfloat16), "ctx", scatter_dimension=0, tiled=True
    ).astype(jnp.float32)
    out_rows = out_four.reshape(shard_rows, kv_heads * group_size * HD)
    query_rows = grad_q.reshape(shard_rows, kv_heads * group_size * HD)
    key_rows = kv_grad[:, : kv_heads * HD]
    value_rows = kv_grad[:, kv_heads * HD :]
    attended, query_grad, key_grad, value_grad = (
        lax.all_to_all(
            out_rows.astype(jnp.bfloat16), "tp", split_axis=0, concat_axis=1, tiled=True
        ).astype(out_rows.dtype),
        lax.all_to_all(
            query_rows.astype(jnp.bfloat16), "tp", split_axis=0, concat_axis=1, tiled=True
        ).astype(query_rows.dtype),
        lax.all_to_all(
            key_rows.astype(jnp.bfloat16), "tp", split_axis=0, concat_axis=1, tiled=True
        ).astype(key_rows.dtype),
        lax.all_to_all(
            value_rows.astype(jnp.bfloat16), "tp", split_axis=0, concat_axis=1, tiled=True
        ).astype(value_rows.dtype),
    )
    return (attended, query_grad, key_grad, value_grad)


def solution(mesh):
    placed = (
        P(("ctx", "tp"), None),
        P(("ctx", "tp"), None),
        P(("ctx", "tp"), None),
        P(("ctx", "tp"), None),
        P(),
    )
    return jax.shard_map(
        per_device,
        mesh=mesh,
        in_specs=placed,
        out_specs=(
            P(("ctx", "tp"), None),
            P(("ctx", "tp"), None),
            P(("ctx", "tp"), None),
            P(("ctx", "tp"), None),
        ),
        check_vma=False,
    )
```

profile of v0, /device:TPU:0, one launch (start us, length us, event | category | flops | bytes accessed | tf_op | source)
XLA Modules:
  0.0 559.3 jit_solution(10896135098754216869)
XLA Ops:
  8.0 15.5 %all_to_all.116 = bf16[32,8,128]{2,0,1:T(8,128)(2,1)} all-to-all(bf16[32,8,128]{2,0,1:T(8,128)(2,1)S(1)} %copy_bitcast_fusion.5), channel_id=1, replica_groups=mesh['ctx'=16,'tp'=8] {'tp'}, dimensions={1} | all-to-all | bytes 131072 | tf_op jit(solution)/shard_map/all_to_all | solution.py:15
  24.5 10.8 %all_to_all.117 = bf16[32,8,128]{2,0,1:T(8,128)(2,1)} all-to-all(bf16[32,8,128]{2,0,1:T(8,128)(2,1)S(1)} %copy_bitcast_fusion.4), channel_id=1, replica_groups=mesh['ctx'=16,'tp'=8] {'tp'}, dimensions={1} | all-to-all | bytes 131072 | tf_op jit(solution)/shard_map/all_to_all | solution.py:16
  35.3 1.9 copy.103
  37.2 3.5 all-to-all-start.1
  41.6 9.0 %all-to-all-done.1 = bf16[32,8,1024]{2,0,1:T(8,128)(2,1)S(1)} async-done(((bf16[32,8,1024]{2,0,1:T(8,128)(2,1)}), bf16[32,8,1024]{2,0,1:T(8,128)(2,1)S(1)}, u32[]{:S(2)}, u32[]{:S(2)}) %all-to-all-start.1) | async-done | bytes 524320 | tf_op jit(solution)/shard_map/all_to_all | solution.py:14
  50.6 3.5 all-to-all-start.4
  55.1 8.6 %all-to-all-done.4 = bf16[32,8,1024]{2,0,1:T(8,128)(2,1)S(1)} async-done(((bf16[32,8,1024]{2,0,1:T(8,128)(2,1)}), bf16[32,8,1024]{2,0,1:T(8,128)(2,1)S(1)}, u32[]{:S(2)}, u32[]{:S(2)}) %all-to-all-start.4) | async-done | bytes 524320 | tf_op jit(solution)/shard_map/all_to_all | solution.py:17
  63.9 70.8 %while.55 = (s32[]{:T(128)}, f32[1,8,256]{2,1,0:T(8,128)S(1)}, f32[1,8,256]{2,1,0:T(8,128)S(1)}, s32[16]{0:T(128)S(1)}, s32[]{:T(128)}, /*index=5*/s32[4096]{0:T...) while((s32[]{:T(128)}, f32[1,8,256]{2,1,0:T(8,128)S(1)}, ...), condition=%wide.region_5.6_spmd.clone, body=%wide.region_0.5_spmd.clone.sunk | while | flops 138613264 | bytes 5098407 | solution.py:70
  68.2 2.9 conditional.9
  134.8 76.3 %while.56 = (s32[]{:T(128)}, f32[1,8,256,128]{3,2,1,0:T(8,128)S(1)}, s32[16]{0:T(128)S(1)}, s32[]{:T(128)}, s32[4096]{0:T(1024)}, /*index=5*/s32[256]{0:T(256)S(...) while((s32[]{:T(128)}, ...), condition=%wide.region_9.10_spmd.clone, body=%wide.region_6.9_spmd.clone.sunk | while | flops 271516160 | bytes 2903447 | solution.py:99
  136.8 1.3 dynamic_slice.160
  139.4 3.1 conditional.10
  140.3 2.1 fusion.17
  144.4 1.3 dynamic_slice.160
  148.9 1.3 dynamic_slice.160
  153.5 1.3 dynamic_slice.160
  158.1 1.3 dynamic_slice.160
  162.7 1.3 dynamic_slice.160
  167.3 1.3 dynamic_slice.160
  185.6 1.3 dynamic_slice.160
  212.0 88.6 %while.57 = (s32[]{:T(128)}, f32[256,1,8,128]{0,3,2,1:T(8,128)S(1)}, bf16[16,256,256]{2,1,0:T(8,128)(2,1)}, s32[16]{0:T(128)S(1)}, s32[]{:T(128)}, /*index=5*/s3...) while((s32[]{:T(128)}, ...), condition=%wide.region_14.15_spmd.clone, body=%wide.region_11.14_spmd.clone.sunk | while | flops 676332032 | bytes 14381519 | solution.py:151
  216.4 5.9 %conditional.11 = (f32[256,1,8,128]{0,3,2,1:T(8,128)S(1)}, bf16[256,128]{1,0:T(8,128)(2,1)S(1)}, bf16[256,128]{1,0:T(8,128)(2,1)S(1)}) conditional(s32[]{:T(128)} %convert_element_type.167, f32[256,1,8,128]{0,3,2,1:T(8,128)S(1)} %get-tuple-element.1630, (bf16[16,256,1,128]{3,1,2,0:T(8,128)(2,1)}, s32[]{:T(128)}, s32[]{:T(128)}, s32[]{:T(128)}, ...), branch_computations={%region_12.12_spmd, %region_13.13_spmd} | conditional | flops 676069888 | bytes 14117424 | solution.py:145
  217.4 1.5 fusion.40
  302.3 3.5 all-to-all-start.3
  307.2 8.2 %all-to-all-done.3 = bf16[8,32,1024]{2,1,0:T(8,128)(2,1)S(1)} async-done(((bf16[8,32,1024]{2,1,0:T(8,128)(2,1)}), bf16[8,32,1024]{2,1,0:T(8,128)(2,1)S(1)}, u32[]{:S(2)}, u32[]{:S(2)}) %all-to-all-start.3) | async-done | bytes 524320 | tf_op jit(solution)/shard_map/all_to_all | solution.py:168
  315.3 3.5 all-to-all-start.5
  319.0 206.5 %reduce-scatter.2.cloned.1.call-done = bf16[256,256]{1,0:T(8,128)(2,1)} async-done(((bf16[4096,256]{1,0:T(8,128)(2,1)}), bf16[256,256]{1,0:T(8,128)(2,1)}) %reduce-scatter.2.cloned.1.call-update) | async-done | bytes 131088 | tf_op jit(solution)/shard_map/reduce_scatter | solution.py:160
  525.5 1.5 fusion.62
  527.0 6.2 %all-to-all-start.7 = ((bf16[8,32,128]{2,1,0:T(8,128)(2,1)}), bf16[8,32,128]{2,1,0:T(8,128)(2,1)S(1)}, u32[]{:S(2)}, u32[]{:S(2)}) async-start(bf16[8,32,128]{2,1,0:T(8,128)(2,1)} %bitcast.53), calls=%async_computation.8 | async-start | bytes 131072 | tf_op jit(solution)/shard_map/all_to_all | solution.py:177
  535.5 5.5 all-to-all-done.7
  541.1 3.4 all-to-all-start.6
  545.1 7.0 %all-to-all-done.6 = bf16[8,32,128]{2,1,0:T(8,128)(2,1)S(1)} async-done(((bf16[8,32,128]{2,1,0:T(8,128)(2,1)}), bf16[8,32,128]{2,1,0:T(8,128)(2,1)S(1)}, u32[]{:S(2)}, u32[]{:S(2)}) %all-to-all-start.6) | async-done | bytes 65568 | tf_op jit(solution)/shard_map/all_to_all | solution.py:174
  (336 shorter events, 140.2 us)
Async XLA Ops:
  7.2 0.8 copy-start
  7.2 33.5 %copy-start.1 = (bf16[32,8192]{1,0:T(8,128)(2,1)S(1)}, bf16[32,8192]{1,0:T(8,128)(2,1)}, u32[]{:S(2)}) copy-start(bf16[32,8192]{1,0:T(8,128)(2,1)} %param.20) | copy-start | bytes 1572868
  7.2 56.7 %all-gather.3.cloned.1.call-start = ((), (), s32[]{:S(2)}) async-start(), calls=%async_computation.9 | async-start | bytes 1114112 | tf_op jit(solution)/shard_map/all_gather | solution.py:77
  23.6 111.2 %all-gather.5.cloned.1.call-start = ((), (), s32[]{:S(2)}) async-start(), calls=%async_computation.10 | async-start | bytes 1114112 | tf_op jit(solution)/shard_map/all_gather | solution.py:78
  37.2 13.4 %all-to-all-start.1 = ((bf16[32,8,1024]{2,0,1:T(8,128)(2,1)}), bf16[32,8,1024]{2,0,1:T(8,128)(2,1)S(1)}, u32[]{:S(2)}, u32[]{:S(2)}) async-start(bf16[32,8,1024]{2,0,1:T(8,128)(2,1)} %bitcast.216), calls=%async_computation.1 | async-start | bytes 1048576 | tf_op jit(solution)/shard_map/all_to_all | solution.py:14
  50.6 13.1 %all-to-all-start.4 = ((bf16[32,8,1024]{2,0,1:T(8,128)(2,1)}), bf16[32,8,1024]{2,0,1:T(8,128)(2,1)S(1)}, u32[]{:S(2)}, u32[]{:S(2)}) async-start(bf16[32,8,1024]{2,0,1:T(8,128)(2,1)} %bitcast.215), calls=%async_computation.4 | async-start | bytes 1048576 | tf_op jit(solution)/shard_map/all_to_all | solution.py:17
  54.1 471.4 %reduce-scatter.2.cloned.1.call-start = ((), (), s32[]{:S(2)}) async-start(), calls=%async_computation.11 | async-start | bytes 2228224 | tf_op jit(solution)/shard_map/reduce_scatter | solution.py:160
  302.3 13.1 %all-to-all-start.3 = ((bf16[8,32,1024]{2,1,0:T(8,128)(2,1)}), bf16[8,32,1024]{2,1,0:T(8,128)(2,1)S(1)}, u32[]{:S(2)}, u32[]{:S(2)}) async-start(bf16[8,32,1024]{2,1,0:T(8,128)(2,1)} %convert_element_type.113), calls=%async_computation.3 | async-start | bytes 1048576 | tf_op jit(solution)/shard_map/all_to_all | solution.py:168
  315.3 211.7 %all-to-all-start.5 = ((bf16[8,32,1024]{2,1,0:T(8,128)(2,1)}), bf16[8,32,1024]{2,1,0:T(8,128)(2,1)S(1)}, u32[]{:S(2)}, u32[]{:S(2)}) async-start(bf16[8,32,1024]{2,1,0:T(8,128)(2,1)} %convert_element_type.119), calls=%async_computation.5 | async-start | bytes 1048576 | tf_op jit(solution)/shard_map/all_to_all | solution.py:171
  527.0 14.0 %all-to-all-start.7 = ((bf16[8,32,128]{2,1,0:T(8,128)(2,1)}), bf16[8,32,128]{2,1,0:T(8,128)(2,1)S(1)}, u32[]{:S(2)}, u32[]{:S(2)}) async-start(bf16[8,32,128]{2,1,0:T(8,128)(2,1)} %bitcast.53), calls=%async_computation.8 | async-start | bytes 131072 | tf_op jit(solution)/shard_map/all_to_all | solution.py:177
  541.1 11.0 %all-to-all-start.6 = ((bf16[8,32,128]{2,1,0:T(8,128)(2,1)}), bf16[8,32,128]{2,1,0:T(8,128)(2,1)S(1)}, u32[]{:S(2)}, u32[]{:S(2)}) async-start(bf16[8,32,128]{2,1,0:T(8,128)(2,1)} %bitcast.51), calls=%async_computation.7 | async-start | bytes 131072 | tf_op jit(solution)/shard_map/all_to_all | solution.py:174
Sparse Core Ops, SparseCore 0:
  23.7 31.1 all-gather.2
  56.6 35.5 all-gather.4
  300.7 224.7 reduce-scatter.1
where the time goes:
time: 568 us; the launch traced here: 559 us
  waiting for transfers between devices  245 us (43%)
  local copies, waits for them, and re-layouts  134 us (24%)
  loops' own time  93.9 us (17%)
  blocking collectives  26.4 us (5%)
  starting transfers between devices  23.7 us (4%)
  other arithmetic  14 us (2%)
  between operations  14 us (2%)
  matrix products  8.31 us (1%)
    reduce_scatter x1, waiting for transfers between devices, per_device(): lax.psum_scatter(kv_buffer.astype(jnp.bfloat16), 'ctx', scatter_dimension...  207 us
    dynamic_slice x48, local copies, waits for them, and re-layouts, active(): doc_last = lax.dynamic_index_in_dim(doc_ids, last_key, 0, keepdims=False)  62.6 us
    another operation x1, loops' own time, per_device(): lax.scan(mix_advance, weighted, (key_blocks, value_blocks, jnp.arange(blo...  32 us
    another operation x1, loops' own time, per_device(): lax.scan(backward_advance, backward_grad_q, (key_blocks, value_blocks, jn...  31.3 us
    dynamic_slice x48, local copies, waits for them, and re-layouts, per_device(): lax.scan(stats_advance, stat_start, (key_blocks, jnp.arange(block_count,...  30 us
    another operation x1, loops' own time, per_device(): lax.scan(stats_advance, stat_start, (key_blocks, jnp.arange(block_count,...  29.4 us
    slice x48, local copies, waits for them, and re-layouts, active(): return (kstart >= 0) & (kstart <= q_last) & (doc_last >= q_doc[0])  26.4 us
    all_to_all x1, blocking collectives, per_device(): lax.all_to_all(keys, 'tp', split_axis=1, concat_axis=0, tiled=True)  15.5 us
  transfers between devices with their start and end apart: 9, of which 6 were waited for; matrix products, arithmetic and copies ran while one was open for 10% of the time, Pallas kernels for 0%

commit v1 on v0

v1 whole, which is shorter than its diff:
```python
import math

import jax
import jax.numpy as jnp
from jax import lax
from jax.experimental import pallas as pl
from jax.experimental.pallas import tpu as pltpu
from jax.sharding import PartitionSpec as P

HD = 128
GROUP = 8
KV = 8
DEV = 128
HALF = 16
PIECE = (HALF, HD)
BLOCKS = 8
ROWS = 256
KEYS = 512
SPAN = ROWS // HALF
TOKENS_BLOCK = 512
SCALE = HD**-0.5
LOG2E = math.log2(math.e)
VERY_LOW = -1e30
NT = (((1,), (1,)), ((), ()))
MIB = 1 << 20


def mm(a, b):
    return jnp.dot(a, b, preferred_element_type=jnp.float32)


def mm_nt(a, b):
    return lax.dot_general(a, b, NT, preferred_element_type=jnp.float32)


def pack_kernel(q_ref, g_ref, k_ref, v_ref, out_ref):
    for hh in range(GROUP):
        for s in range(2):
            rows = slice(s * HALF, (s + 1) * HALF)
            for g in range(KV):
                to = (hh * 2 + s) * KV + g
                head = slice((g * GROUP + hh) * HD, (g * GROUP + hh + 1) * HD)
                group = slice(g * HD, (g + 1) * HD)
                out_ref[to, 0] = q_ref[rows, head]
                out_ref[to, 1] = g_ref[rows, head]
                out_ref[to, 2] = k_ref[rows, group]
                out_ref[to, 3] = v_ref[rows, group]


def attention_kernel(
    info_ref, got_ref, far_ref,
    odq_ref, own_ref, oth_ref,
    k_all, v_all, k_t, v_t, dk_acc, dv_acc, s_all, top, tot, o_t, dq_t,
):
    first_1, first_2, first_3, half = info_ref[0], info_ref[1], info_ref[2], info_ref[3]

    def doc_start(token):
        start = jnp.where(token >= first_1, first_1, 0)
        start = jnp.where(token >= first_2, first_2, start)
        return jnp.where(token >= first_3, first_3, start)

    def spread(r):
        return r + (r & ~(HALF - 1))

    def gather(j, carry):
        span = pl.ds(j * SPAN, SPAN)
        k_all[j, :ROWS] = got_ref[span, 2].reshape(ROWS, HD)
        k_all[j, ROWS:] = far_ref[span, 0].reshape(ROWS, HD)
        v_all[j, :ROWS] = got_ref[span, 3].reshape(ROWS, HD)
        v_all[j, ROWS:] = far_ref[span, 1].reshape(ROWS, HD)
        k_t[j] = k_all[j].T
        v_t[j] = v_all[j].T
        dk_acc[j] = jnp.zeros((KEYS, HD), jnp.float32)
        dv_acc[j] = jnp.zeros((KEYS, HD), jnp.float32)
        return carry

    lax.fori_loop(0, BLOCKS, gather, 0)

    def block(i, carry):
        span = pl.ds(i * SPAN, SPAN)
        q = got_ref[span, 0].reshape(ROWS, HD)
        g = got_ref[span, 1].reshape(ROWS, HD)
        first = i * TOKENS_BLOCK
        lo = doc_start(first) // TOKENS_BLOCK
        last_start = doc_start(first + TOKENS_BLOCK - 1)
        top[...] = jnp.full((8, ROWS), VERY_LOW, jnp.float32)

        def score(j, carry):
            def step(masked):
                s = mm_nt(k_all[j], q)
                if masked:
                    q_tok = first + HALF * half + spread(
                        lax.broadcasted_iota(jnp.int32, (1, ROWS), 1)
                    )
                    r = lax.broadcasted_iota(jnp.int32, (KEYS, ROWS), 0)
                    far = r >= ROWS
                    r = jnp.where(far, r - ROWS, r)
                    k_half = jnp.where(far, 1 - half, half)
                    k_tok = j * TOKENS_BLOCK + spread(r) + HALF * k_half
                    s = jnp.where((k_tok <= q_tok) & (k_tok >= doc_start(q_tok)), s, VERY_LOW)
                s_all[j] = s
                top[...] = jnp.maximum(top[...], jnp.max(s.reshape(KEYS // 8, 8, ROWS), axis=0))

            masked = (j == i) | (j * TOKENS_BLOCK < last_start)
            pl.when(masked)(lambda: step(True))
            pl.when(jnp.logical_not(masked))(lambda: step(False))
            return carry

        lax.fori_loop(lo, i + 1, score, 0)
        shift = jnp.max(top[...], axis=0, keepdims=True) * (SCALE * LOG2E)
        tot[...] = jnp.zeros((8, ROWS), jnp.float32)
        o_t[...] = jnp.zeros((HD, ROWS), jnp.float32)

        def mix(j, carry):
            e = jnp.exp2(s_all[j] * (SCALE * LOG2E) - shift)
            s_all[j] = e
            tot[...] += jnp.sum(e.reshape(KEYS // 8, 8, ROWS), axis=0)
            o_t[...] += mm(v_t[j], e.astype(jnp.bfloat16))
            return carry

        lax.fori_loop(lo, i + 1, mix, 0)
        inverse = 1.0 / jnp.sum(tot[...], axis=0, keepdims=True)
        o = (o_t[...] * inverse).T
        odq_ref[span, 0] = o.astype(jnp.bfloat16).reshape(SPAN, *PIECE)
        delta = jnp.sum((g.astype(jnp.float32) * o).T, axis=0, keepdims=True)
        dq_t[...] = jnp.zeros((HD, ROWS), jnp.float32)

        def back(j, carry):
            prob = s_all[j] * inverse
            d_prob = mm_nt(v_all[j], g)
            d_score = (prob * (d_prob - delta)).astype(jnp.bfloat16)
            dv_acc[j] += mm(prob.astype(jnp.bfloat16), g)
            dk_acc[j] += mm(d_score, q)
            dq_t[...] += mm(k_t[j], d_score)
            return carry

        lax.fori_loop(lo, i + 1, back, 0)
        odq_ref[span, 1] = (dq_t[...] * SCALE).T.astype(jnp.bfloat16).reshape(SPAN, *PIECE)
        return carry

    lax.fori_loop(0, BLOCKS, block, 0)

    def give(j, carry):
        span = pl.ds(j * SPAN, SPAN)
        own_ref[span, 0] = (dk_acc[j, :ROWS] * SCALE).reshape(SPAN, *PIECE)
        own_ref[span, 1] = dv_acc[j, :ROWS].reshape(SPAN, *PIECE)
        oth_ref[span, 0] = (dk_acc[j, ROWS:] * SCALE).astype(jnp.bfloat16).reshape(SPAN, *PIECE)
        oth_ref[span, 1] = dv_acc[j, ROWS:].astype(jnp.bfloat16).reshape(SPAN, *PIECE)
        return carry

    lax.fori_loop(0, BLOCKS, give, 0)


def unpack_kernel(got_ref, o_ref, dq_ref, dk_ref, dv_ref):
    for s in range(2):
        rows = slice(s * HALF, (s + 1) * HALF)
        for g in range(KV):
            group = slice(g * HD, (g + 1) * HD)
            dk = jnp.zeros(PIECE, jnp.float32)
            dv = jnp.zeros(PIECE, jnp.float32)
            for hh in range(GROUP):
                at = (hh * 2 + s) * KV + g
                head = slice((g * GROUP + hh) * HD, (g * GROUP + hh + 1) * HD)
                o_ref[rows, head] = got_ref[at, 0].astype(jnp.float32)
                dq_ref[rows, head] = got_ref[at, 1].astype(jnp.float32)
                dk += got_ref[at, 2].astype(jnp.float32)
                dv += got_ref[at, 3].astype(jnp.float32)
            dk_ref[rows, group] = dk
            dv_ref[rows, group] = dv


def everyone(x):
    return lax.all_to_all(x, ("ctx", "tp"), 0, 0, tiled=True)


def swap_cores(x):
    return lax.ppermute(x, "ctx", [(c, c ^ 1) for c in range(16)])


def per_device(queries, keys, values, out_grad, doc_ids):
    bf16, f32 = jnp.bfloat16, jnp.float32
    sent = pl.pallas_call(
        pack_kernel,
        out_shape=jax.ShapeDtypeStruct((DEV, 4, *PIECE), bf16),
        compiler_params=pltpu.CompilerParams(vmem_limit_bytes=32 * MIB),
    )(queries, out_grad, keys, values)
    got = everyone(sent)
    far = swap_cores(got[:, 2:])
    firsts = jnp.sum(doc_ids[None, :] < jnp.arange(1, 4, dtype=jnp.int32)[:, None], axis=1)
    half = lax.axis_index("ctx") % 2
    info = jnp.concatenate([firsts.astype(jnp.int32), half.astype(jnp.int32)[None]])
    pair = (DEV, 2, *PIECE)
    odq, own, oth = pl.pallas_call(
        attention_kernel,
        out_shape=(
            jax.ShapeDtypeStruct(pair, bf16),
            jax.ShapeDtypeStruct(pair, f32),
            jax.ShapeDtypeStruct(pair, bf16),
        ),
        in_specs=[
            pl.BlockSpec(memory_space=pltpu.SMEM),
            pl.BlockSpec(memory_space=pltpu.VMEM),
            pl.BlockSpec(memory_space=pltpu.VMEM),
        ],
        scratch_shapes=[
            pltpu.VMEM((BLOCKS, KEYS, HD), bf16),
            pltpu.VMEM((BLOCKS, KEYS, HD), bf16),
            pltpu.VMEM((BLOCKS, HD, KEYS), bf16),
            pltpu.VMEM((BLOCKS, HD, KEYS), bf16),
            pltpu.VMEM((BLOCKS, KEYS, HD), f32),
            pltpu.VMEM((BLOCKS, KEYS, HD), f32),
            pltpu.VMEM((BLOCKS, KEYS, ROWS), f32),
            pltpu.VMEM((8, ROWS), f32),
            pltpu.VMEM((8, ROWS), f32),
            pltpu.VMEM((HD, ROWS), f32),
            pltpu.VMEM((HD, ROWS), f32),
        ],
        compiler_params=pltpu.CompilerParams(vmem_limit_bytes=48 * MIB),
    )(info, got, far)
    dkv = (own + swap_cores(oth).astype(f32)).astype(bf16)
    back = everyone(jnp.concatenate([odq, dkv], axis=1))
    return pl.pallas_call(
        unpack_kernel,
        out_shape=(
            jax.ShapeDtypeStruct((2 * HALF, KV * GROUP * HD), f32),
            jax.ShapeDtypeStruct((2 * HALF, KV * GROUP * HD), f32),
            jax.ShapeDtypeStruct((2 * HALF, KV * HD), f32),
            jax.ShapeDtypeStruct((2 * HALF, KV * HD), f32),
        ),
        compiler_params=pltpu.CompilerParams(vmem_limit_bytes=32 * MIB),
    )(back)


def solution(mesh):
    rows = P(("ctx", "tp"), None)
    return jax.shard_map(
        per_device,
        mesh=mesh,
        in_specs=(rows, rows, rows, rows, P()),
        out_specs=(rows, rows, rows, rows),
        check_vma=False,
    )
```

time: 568 us -> 128 us (0.23); the launches traced: 559 us -> 127 us
  waiting for transfers between devices: 245 us -> 5.1 us
  local copies, waits for them, and re-layouts: 134 us -> 4.97 us
  loops' own time: 93.9 us -> 0 us
  blocking collectives: 26.4 us -> 74.1 us
  Pallas kernels: 0 us -> 41.2 us
  starting transfers between devices: 23.7 us -> 0.21 us
  between operations: 14 us -> 0.67 us
  other arithmetic: 14 us -> 0.87 us
  matrix products: 8.31 us -> 0 us
    reduce_scatter x1 -> x0, waiting for transfers between devices: 207 us -> none  [per_device(): lax.psum_scatter(kv_buffer.astype(jnp.bfloat16), 'ctx', scatter_dimension...]
    dynamic_slice x100 -> x0, local copies, waits for them, and re-layouts: 95.7 us -> none  [the longest x48 62.6 us: active(): doc_last = lax.dynamic_index_in_dim(doc_ids, last_key, 0, keepdims=False)]
    another operation x51 -> x0, loops' own time: 93.9 us -> none  [the longest x1 32 us: per_device(): lax.scan(mix_advance, weighted, (key_blocks, value_blocks, jnp.arange(blo...]
    all_to_all x2, blocking collectives: 26.4 us -> 74.1 us  [everyone(): return lax.all_to_all(x, ('ctx', 'tp'), 0, 0, tiled=True)]
    pallas_call x0 -> x3, Pallas kernels: none -> 41.2 us  [the longest x1 39.4 us: per_device(): pl.pallas_call(attention_kernel, out_shape=(jax.ShapeDtypeStruct(pair, bf...]
    all_to_all x6 -> x0, waiting for transfers between devices: 38.3 us -> none  [the longest x1 9.03 us: per_device(): lax.all_to_all(queries, 'tp', split_axis=1, concat_axis=0, tiled=True)]
    slice x49 -> x1, local copies, waits for them, and re-layouts: 27.9 us -> 1.21 us  [per_device(): far = swap_cores(got[:, 2:])]
    all_to_all x6 -> x0, starting transfers between devices: 23.6 us -> none  [the longest x1 6.24 us: per_device(): lax.all_to_all(value_rows.astype(jnp.bfloat16), 'tp', split_axis=0, conca...]
  transfers between devices with their start and end apart: 9 -> 2, of which waited for: 6 -> 2; matrix products, arithmetic and copies ran while one was open for 10% -> 0% of each run, Pallas kernels for 0% -> 0%
where the time goes in v1:
time: 128 us; the launch traced here: 127 us
  blocking collectives  74.1 us (58%)
  Pallas kernels  41.2 us (32%)
  waiting for transfers between devices  5.1 us (4%)
  local copies, waits for them, and re-layouts  4.97 us (4%)
    all_to_all x2, blocking collectives, everyone(): return lax.all_to_all(x, ('ctx', 'tp'), 0, 0, tiled=True)  74.1 us
    pallas_call x1, Pallas kernels, per_device(): pl.pallas_call(attention_kernel, out_shape=(jax.ShapeDtypeStruct(pair, bf...  39.4 us
    ppermute x2, waiting for transfers between devices, swap_cores(): return lax.ppermute(x, 'ctx', [(c, c ^ 1) for c in range(16)])  5.1 us
    unnamed x12, local copies, waits for them, and re-layouts  3.76 us
  transfers between devices with their start and end apart: 2, of which 2 were waited for; matrix products, arithmetic and copies ran while one was open for 0% of the time, Pallas kernels for 0%

profile of v1, /device:TPU:0, one launch (start us, length us, event | category | flops | bytes accessed | tf_op | source)
XLA Modules:
  0.0 127.1 jit_solution(362926211894451359)
XLA Ops:
  0.6 0.0 copy-start
  0.6 1.0 copy-done
  1.7 0.0 copy-start.1
  1.7 1.0 copy-done.1
  2.7 0.0 copy-start.2
  2.7 0.8 copy-done.2
  3.6 0.0 copy-start.3
  3.6 0.8 copy-done.3
  4.4 0.3 shard_map.84
  4.7 39.6 %all_to_all.10.got_ref = bf16[128,4,16,128]{3,2,1,0:T(8,128)(2,1)S(1)} all-to-all(bf16[128,4,16,128]{3,2,1,0:T(8,128)(2,1)S(1)} %shard_map.84), channel_id=1, replica_groups=mesh['ctx'=16,'tp'=8] {'ctx','tp'}, dimensions={0} | all-to-all | bytes 4194304 | tf_op jit(solution)/shard_map/all_to_all | solution.py:173
  44.4 0.0 copy-start.4
  44.4 0.0 copy-start.5
  44.4 1.2 slice.4
  45.6 0.0 collective-permute-start
  45.6 0.0 copy-done.5
  45.6 0.2 convert_reduce_fusion
  45.8 0.1 pad_add_fusion.info_ref
  45.9 2.6 %collective-permute-done.far_ref = bf16[128,2,16,128]{3,2,1,0:T(8,128)(2,1)S(1)} collective-permute-done((bf16[128,2,16,128]{3,2,1,0:T(8,128)(2,1)}, bf16[128,2,16,128]{3,2,1,0:T(8,128)(2,1)S(1)}, u32[]{:S(2)}, u32[]{:S(2)}) %collective-permute-start) | collective-permute-done | bytes 1048608 | tf_op jit(solution)/shard_map/ppermute | solution.py:177
  48.4 0.0 copy-done.4
  48.4 39.4 %shard_map.85 = (bf16[128,2,16,128]{3,2,1,0:T(8,128)(2,1)S(1)}, f32[128,2,16,128]{3,2,1,0:T(8,128)S(1)}, bf16[128,2,16,128]{3,2,1,0:T(8,128)(2,1)S(1)}) custom-call(s32[4]{0:T(128)S(1)} %pad_add_fusion.info_ref, bf16[128,4,16,128]{3,2,1,0:T(8,128)(2,1)} %copy-done.4, bf16[128,2,16,128]{3,2,1,0:T(8,128)(2,1)S(1)} %collective-permute-done.far_ref), custom_call_target="tpu_custom_call" | custom-call | tf_op jit(solution)/shard_map/pallas_call | solution.py:193
  87.8 0.2 collective-permute-start.1
  88.0 2.5 %collective-permute-done.1 = bf16[128,2,16,128]{3,2,1,0:T(8,128)(2,1)S(1)} collective-permute-done((bf16[128,2,16,128]{3,2,1,0:T(8,128)(2,1)S(1)}, bf16[128,2,16,128]{3,2,1,0:T(8,128)(2,1)S(1)}, u32[]{:S(2)}, u32[]{:S(2)}) %collective-permute-start.1) | collective-permute-done | bytes 1048608 | tf_op jit(solution)/shard_map/ppermute | solution.py:177
  90.6 0.4 add_convert_fusion
  91.0 0.2 pad_maximum_fusion
  91.2 34.4 %all_to_all.11.got_ref = bf16[128,4,16,128]{3,2,1,0:T(8,128)(2,1)S(1)} all-to-all(bf16[128,4,16,128]{3,2,1,0:T(8,128)(2,1)S(1)} %pad_maximum_fusion), channel_id=1, replica_groups=mesh['ctx'=16,'tp'=8] {'ctx','tp'}, dimensions={0} | all-to-all | bytes 4194304 | tf_op jit(solution)/shard_map/all_to_all | solution.py:173
  125.6 1.5 %shard_map.86 = (f32[32,8192]{1,0:T(8,128)}, f32[32,8192]{1,0:T(8,128)}, f32[32,1024]{1,0:T(8,128)}, f32[32,1024]{1,0:T(8,128)}) custom-call(bf16[128,4,16,128]{3,2,1,0:T(8,128)(2,1)S(1)} %all_to_all.11.got_ref), custom_call_target="tpu_custom_call" | custom-call | tf_op jit(solution)/shard_map/pallas_call | solution.py:222
  (1 shorter events, 0.0 us)
Async XLA Ops:
  0.6 1.0 copy-start
  1.7 1.0 copy-start.1
  2.7 0.8 copy-start.2
  3.6 0.8 copy-start.3
  44.4 4.1 %copy-start.4 = (bf16[128,4,16,128]{3,2,1,0:T(8,128)(2,1)}, bf16[128,4,16,128]{3,2,1,0:T(8,128)(2,1)S(1)}, u32[]{:S(2)}) copy-start(bf16[128,4,16,128]{3,2,1,0:T(8,128)(2,1)S(1)} %all_to_all.10.got_ref) | copy-start | bytes 6291460
  44.4 1.2 copy-start.5
  45.6 2.9 %collective-permute-start = (bf16[128,2,16,128]{3,2,1,0:T(8,128)(2,1)}, bf16[128,2,16,128]{3,2,1,0:T(8,128)(2,1)S(1)}, u32[]{:S(2)}, u32[]{:S(2)}) collective-permute-start(bf16[128,2,16,128]{3,2,1,0:T(8,128)(2,1)} %slice.4), channel_id=1, source_target_pairs={{0,8},{8,0},{16,24},{24,16},{32,40},{40,32},{48,56},{56,48},{64,72... | collective-permute-start | bytes 3145736 | tf_op jit(solution)/shard_map/ppermute | solution.py:177
  87.8 2.7 %collective-permute-start.1 = (bf16[128,2,16,128]{3,2,1,0:T(8,128)(2,1)S(1)}, bf16[128,2,16,128]{3,2,1,0:T(8,128)(2,1)S(1)}, u32[]{:S(2)}, u32[]{:S(2)}) collective-permute-start(bf16[128,2,16,128]{3,2,1,0:T(8,128)(2,1)S(1)} %get-tuple-element.9), channel_id=1, source_target_pairs={{0,8},{8,0},{16,24},{24,16},{32,40},{40,32},{48,56},{56,48},{64,72... | collective-permute-start | bytes 3145736 | tf_op jit(solution)/shard_map/ppermute | solution.py:177

commit v2 on v1

v2 whole, which is shorter than its diff:
```python
import math

import jax
import jax.numpy as jnp
from jax import lax
from jax.experimental import pallas as pl
from jax.experimental.pallas import tpu as pltpu
from jax.sharding import PartitionSpec as P

HD = 128
GROUP = 8
KV = 8
DEV = 128
HALF = 16
PIECE = (HALF, HD)
TOKENS = 4096
ROWS_ALL = TOKENS // 2
ROWS = 512
FAR = 512
TILE = 256
BLOCKS = ROWS_ALL // ROWS
CHUNKS = ROWS_ALL // FAR
KEYS = 2 * FAR
ROW_SPAN = ROWS // HALF
KEY_SPAN = FAR // HALF
SCALE = HD**-0.5
LOG2E = math.log2(math.e)
VERY_LOW = -1e30
NT = (((1,), (1,)), ((), ()))
MIB = 1 << 20


def mm(a, b):
    return jnp.dot(a, b, preferred_element_type=jnp.float32)


def mm_nt(a, b):
    return lax.dot_general(a, b, NT, preferred_element_type=jnp.float32)


def pack_kernel(q_hbm, g_hbm, k_hbm, v_hbm, out_hbm, q_ref, g_ref, k_ref, v_ref, out_ref, sems):
    arrays = ((q_hbm, q_ref), (g_hbm, g_ref), (k_hbm, k_ref), (v_hbm, v_ref))
    arrived, left = [], []
    for g in range(KV):
        for n, (src, dst) in enumerate(arrays):
            width = src.shape[1] // KV
            columns = pl.ds(g * width, width)
            arrived.append(
                pltpu.make_async_copy(src.at[:, columns], dst.at[:, columns], sems.at[g, n])
            )
            arrived[-1].start()
    for g in range(KV):
        for copy in arrived[4 * g : 4 * g + 4]:
            copy.wait()
        for hh in range(GROUP):
            for s in range(2):
                rows = slice(s * HALF, (s + 1) * HALF)
                head = slice((g * GROUP + hh) * HD, (g * GROUP + hh + 1) * HD)
                group = slice(g * HD, (g + 1) * HD)
                to = hh * 2 + s
                out_ref[to, g, 0] = q_ref[rows, head]
                out_ref[to, g, 1] = g_ref[rows, head]
                out_ref[to, g, 2] = k_ref[rows, group]
                out_ref[to, g, 3] = v_ref[rows, group]
        left.append(pltpu.make_async_copy(out_ref.at[:, g], out_hbm.at[:, g], sems.at[g, 4]))
        left[-1].start()
    for copy in left:
        copy.wait()


def split_kernel(got_ref, own_ref):
    own_ref[...] = got_ref[:, 2:]


def attention_kernel(
    info_ref, got_ref, far_ref,
    odq_ref, own_ref, oth_ref,
    k_all, v_all, k_t, v_t, dk_acc, dv_acc, s_all, top, tot, o_t, dq_t,
):
    first_1, first_2, first_3, half = info_ref[0], info_ref[1], info_ref[2], info_ref[3]

    def doc_start(token):
        start = jnp.where(token >= first_1, first_1, 0)
        start = jnp.where(token >= first_2, first_2, start)
        return jnp.where(token >= first_3, first_3, start)

    def spread(r):
        return r + (r & ~(HALF - 1))

    def gather(j, carry):
        span = pl.ds(j * KEY_SPAN, KEY_SPAN)
        k_all[j, :FAR] = got_ref[span, 2].reshape(FAR, HD)
        k_all[j, FAR:] = far_ref[span, 0].reshape(FAR, HD)
        v_all[j, :FAR] = got_ref[span, 3].reshape(FAR, HD)
        v_all[j, FAR:] = far_ref[span, 1].reshape(FAR, HD)
        k_t[j] = k_all[j].T
        v_t[j] = v_all[j].T
        return carry

    lax.fori_loop(0, CHUNKS, gather, 0)
    tiles = [(h * FAR + t, t, h) for h in range(2) for t in range(0, FAR, TILE)]

    def block(i, carry):
        span = pl.ds(i * ROW_SPAN, ROW_SPAN)
        q = got_ref[span, 0].reshape(ROWS, HD)
        g = got_ref[span, 1].reshape(ROWS, HD)
        g_t = g.T
        first = i * KEYS
        lo = doc_start(first) // KEYS
        last_start = doc_start(first + KEYS - 1)
        q_tok = first + HALF * half + spread(lax.broadcasted_iota(jnp.int32, (1, ROWS), 1))
        q_start = doc_start(q_tok)

        def k_token(j, t, h):
            r = lax.broadcasted_iota(jnp.int32, (TILE, 1), 0)
            return j * KEYS + spread(t + r) + HALF * (half if h == 0 else 1 - half)

        def put_top(s, r0, new):
            m = jnp.max(s.reshape(TILE // 8, 8, ROWS - r0), axis=0)
            top[:, r0:] = m if new else jnp.maximum(top[:, r0:], m)

        for at, t, h in tiles:
            k_tok = k_token(i, t, h)
            s = mm_nt(k_all[i, at : at + TILE], q[t:])
            s = jnp.where((k_tok <= q_tok[:, t:]) & (k_tok >= q_start[:, t:]), s, VERY_LOW)
            s_all[i, at : at + TILE, t:] = s
            put_top(s, t, at == 0)

        def score(j, carry):
            def step(masked):
                for at, t, h in tiles:
                    s = mm_nt(k_all[j, at : at + TILE], q)
                    if masked:
                        s = jnp.where(k_token(j, t, h) >= q_start, s, VERY_LOW)
                    s_all[j, at : at + TILE] = s
                    put_top(s, 0, False)

            masked = j * KEYS < last_start
            pl.when(masked)(lambda: step(True))
            pl.when(jnp.logical_not(masked))(lambda: step(False))
            return carry

        lax.fori_loop(lo, i, score, 0)
        shift = jnp.max(top[...], axis=0, keepdims=True) * (SCALE * LOG2E)

        def mix_tile(j, at, r0):
            e = jnp.exp2(s_all[j, at : at + TILE, r0:] * (SCALE * LOG2E) - shift[:, r0:])
            s_all[j, at : at + TILE, r0:] = e
            e_sum = jnp.sum(e.reshape(TILE // 8, 8, ROWS - r0), axis=0)
            return e_sum, mm(v_t[j, :, at : at + TILE], e.astype(jnp.bfloat16))

        for at, t, h in tiles:
            e_sum, mixed = mix_tile(i, at, t)
            tot[:, t:] = e_sum if at == 0 else tot[:, t:] + e_sum
            o_t[:, t:] = mixed if at == 0 else o_t[:, t:] + mixed

        def mix(j, carry):
            for at, t, h in tiles:
                e_sum, mixed = mix_tile(j, at, 0)
                tot[...] += e_sum
                o_t[...] += mixed
            return carry

        lax.fori_loop(lo, i, mix, 0)
        inverse = 1.0 / jnp.sum(tot[...], axis=0, keepdims=True)
        out_t = o_t[...] * inverse
        odq_ref[span, 0] = out_t.T.astype(jnp.bfloat16).reshape(ROW_SPAN, *PIECE)
        delta = jnp.sum(g_t.astype(jnp.float32) * out_t, axis=0, keepdims=True)

        def back_tile(j, at, r0):
            prob = s_all[j, at : at + TILE, r0:] * inverse[:, r0:]
            d_prob = mm_nt(v_all[j, at : at + TILE], g[r0:])
            d_score = (prob * (d_prob - delta[:, r0:])).astype(jnp.bfloat16)
            return (
                mm(prob.astype(jnp.bfloat16), g[r0:]),
                mm(d_score, q[r0:]),
                mm(k_t[j, :, at : at + TILE], d_score),
            )

        for at, t, h in tiles:
            dv, dk, dq = back_tile(i, at, t)
            dv_acc[i, at : at + TILE] = dv
            dk_acc[i, at : at + TILE] = dk
            dq_t[:, t:] = dq if at == 0 else dq_t[:, t:] + dq

        def back(j, carry):
            for at, t, h in tiles:
                dv, dk, dq = back_tile(j, at, 0)
                dv_acc[j, at : at + TILE] += dv
                dk_acc[j, at : at + TILE] += dk
                dq_t[...] += dq
            return carry

        lax.fori_loop(lo, i, back, 0)
        odq_ref[span, 1] = (dq_t[...] * SCALE).T.astype(jnp.bfloat16).reshape(ROW_SPAN, *PIECE)
        return carry

    lax.fori_loop(0, BLOCKS, block, 0)

    def give(j, carry):
        span = pl.ds(j * KEY_SPAN, KEY_SPAN)
        dk = dk_acc[j] * SCALE
        dv = dv_acc[j]
        own_ref[span, 0] = dk[:FAR].reshape(KEY_SPAN, *PIECE)
        own_ref[span, 1] = dv[:FAR].reshape(KEY_SPAN, *PIECE)
        oth_ref[span, 0] = dk[FAR:].astype(jnp.bfloat16).reshape(KEY_SPAN, *PIECE)
        oth_ref[span, 1] = dv[FAR:].astype(jnp.bfloat16).reshape(KEY_SPAN, *PIECE)
        return carry

    lax.fori_loop(0, CHUNKS, give, 0)


def join_kernel(odq_ref, own_ref, back_ref, out_ref):
    out_ref[:, :2] = odq_ref[...]
    out_ref[:, 2:] = (own_ref[...] + back_ref[...].astype(jnp.float32)).astype(jnp.bfloat16)


def unpack_kernel(got_ref, o_hbm, dq_hbm, dk_hbm, dv_hbm, o_ref, dq_ref, dk_ref, dv_ref, sems):
    copies = []

    def send(src, dst):
        copies.append(pltpu.make_async_copy(src, dst, sems.at[len(copies)]))
        copies[-1].start()

    for g in range(KV):
        group = slice(g * HD, (g + 1) * HD)
        for s in range(2):
            rows = slice(s * HALF, (s + 1) * HALF)
            dk = jnp.zeros(PIECE, jnp.float32)
            dv = jnp.zeros(PIECE, jnp.float32)
            for hh in range(GROUP):
                at = (hh * 2 + s) * KV + g
                head = slice((g * GROUP + hh) * HD, (g * GROUP + hh + 1) * HD)
                o_ref[rows, head] = got_ref[at, 0].astype(jnp.float32)
                dq_ref[rows, head] = got_ref[at, 1].astype(jnp.float32)
                dk += got_ref[at, 2].astype(jnp.float32)
                dv += got_ref[at, 3].astype(jnp.float32)
            dk_ref[rows, group] = dk
            dv_ref[rows, group] = dv
        heads = pl.ds(g * GROUP * HD, GROUP * HD)
        send(o_ref.at[:, heads], o_hbm.at[:, heads])
        send(dq_ref.at[:, heads], dq_hbm.at[:, heads])
    send(dk_ref, dk_hbm)
    send(dv_ref, dv_hbm)
    for copy in copies:
        copy.wait()


def everyone(x):
    return lax.all_to_all(x, ("ctx", "tp"), 0, 0, tiled=True)


def swap_cores(x):
    return lax.ppermute(x, "ctx", [(c, c ^ 1) for c in range(16)])


def per_device(queries, keys, values, out_grad, doc_ids):
    bf16, f32 = jnp.bfloat16, jnp.float32
    wide, narrow = (2 * HALF, KV * GROUP * HD), (2 * HALF, KV * HD)
    hbm = pl.BlockSpec(memory_space=pltpu.HBM)
    packed = (DEV // KV, KV, 4, *PIECE)
    sent = pl.pallas_call(
        pack_kernel,
        out_shape=jax.ShapeDtypeStruct(packed, bf16),
        in_specs=[hbm] * 4,
        out_specs=hbm,
        scratch_shapes=[
            pltpu.VMEM(wide, bf16),
            pltpu.VMEM(wide, bf16),
            pltpu.VMEM(narrow, bf16),
            pltpu.VMEM(narrow, bf16),
            pltpu.VMEM(packed, bf16),
            pltpu.SemaphoreType.DMA((KV, 5)),
        ],
        compiler_params=pltpu.CompilerParams(vmem_limit_bytes=60 * MIB),
    )(queries, out_grad, keys, values).reshape(DEV, 4, *PIECE)
    got = everyone(sent)
    pair = (DEV, 2, *PIECE)
    near = pl.pallas_call(
        split_kernel,
        out_shape=jax.ShapeDtypeStruct(pair, bf16),
        compiler_params=pltpu.CompilerParams(vmem_limit_bytes=16 * MIB),
    )(got)
    far = swap_cores(near)
    firsts = jnp.sum(doc_ids[None, :] < jnp.arange(1, 4, dtype=jnp.int32)[:, None], axis=1)
    half = lax.axis_index("ctx") % 2
    info = jnp.concatenate([firsts.astype(jnp.int32), half.astype(jnp.int32)[None]])
    odq, own, oth = pl.pallas_call(
        attention_kernel,
        out_shape=(
            jax.ShapeDtypeStruct(pair, bf16),
            jax.ShapeDtypeStruct(pair, f32),
            jax.ShapeDtypeStruct(pair, bf16),
        ),
        in_specs=[
            pl.BlockSpec(memory_space=pltpu.SMEM),
            pl.BlockSpec(memory_space=pltpu.VMEM),
            pl.BlockSpec(memory_space=pltpu.VMEM),
        ],
        scratch_shapes=[
            pltpu.VMEM((CHUNKS, KEYS, HD), bf16),
            pltpu.VMEM((CHUNKS, KEYS, HD), bf16),
            pltpu.VMEM((CHUNKS, HD, KEYS), bf16),
            pltpu.VMEM((CHUNKS, HD, KEYS), bf16),
            pltpu.VMEM((CHUNKS, KEYS, HD), f32),
            pltpu.VMEM((CHUNKS, KEYS, HD), f32),
            pltpu.VMEM((CHUNKS, KEYS, ROWS), f32),
            pltpu.VMEM((8, ROWS), f32),
            pltpu.VMEM((8, ROWS), f32),
            pltpu.VMEM((HD, ROWS), f32),
            pltpu.VMEM((HD, ROWS), f32),
        ],
        compiler_params=pltpu.CompilerParams(vmem_limit_bytes=32 * MIB),
    )(info, got, far)
    back = everyone(
        pl.pallas_call(
            join_kernel,
            out_shape=jax.ShapeDtypeStruct((DEV, 4, *PIECE), bf16),
            compiler_params=pltpu.CompilerParams(vmem_limit_bytes=16 * MIB),
        )(odq, own, swap_cores(oth))
    )
    return pl.pallas_call(
        unpack_kernel,
        out_shape=(
            jax.ShapeDtypeStruct(wide, f32),
            jax.ShapeDtypeStruct(wide, f32),
            jax.ShapeDtypeStruct(narrow, f32),
            jax.ShapeDtypeStruct(narrow, f32),
        ),
        out_specs=[hbm] * 4,
        scratch_shapes=[
            pltpu.VMEM(wide, f32),
            pltpu.VMEM(wide, f32),
            pltpu.VMEM(narrow, f32),
            pltpu.VMEM(narrow, f32),
            pltpu.SemaphoreType.DMA((2 * KV + 2,)),
        ],
        compiler_params=pltpu.CompilerParams(vmem_limit_bytes=16 * MIB),
    )(back)


def solution(mesh):
    rows = P(("ctx", "tp"), None)
    return jax.shard_map(
        per_device,
        mesh=mesh,
        in_specs=(rows, rows, rows, rows, P()),
        out_specs=(rows, rows, rows, rows),
        check_vma=False,
    )
```

time: 128 us -> 109 us (0.85)
  Pallas kernels: 41.2 us -> 27.8 us
  local copies, waits for them, and re-layouts: 4.97 us -> 0.53 us
    pallas_call x1, Pallas kernels: 39.4 us -> 23.3 us  [per_device(): pl.pallas_call(attention_kernel, out_shape=(jax.ShapeDtypeStruct(pair, bf...]
    unnamed x12 -> x2, local copies, waits for them, and re-layouts: 3.76 us -> 0.53 us
    pallas_call x2 -> x4, Pallas kernels: 1.82 us -> 4.48 us  [the longest x1 2.61 us: per_device(): pl.pallas_call(pack_kernel, out_shape=jax.ShapeDtypeStruct(packed, bf16),...]
where the time goes in v2:
time: 109 us; the launch traced here: 108 us
  blocking collectives  74.3 us (68%)
  Pallas kernels  27.8 us (26%)
  waiting for transfers between devices  4.44 us (4%)
    all_to_all x2, blocking collectives, everyone(): return lax.all_to_all(x, ('ctx', 'tp'), 0, 0, tiled=True)  74.3 us
    pallas_call x1, Pallas kernels, per_device(): pl.pallas_call(attention_kernel, out_shape=(jax.ShapeDtypeStruct(pair, bf...  23.3 us
    ppermute x2, waiting for transfers between devices, swap_cores(): return lax.ppermute(x, 'ctx', [(c, c ^ 1) for c in range(16)])  4.44 us
    pallas_call x1, Pallas kernels, per_device(): pl.pallas_call(pack_kernel, out_shape=jax.ShapeDtypeStruct(packed, bf16),...  2.61 us
  transfers between devices with their start and end apart: 2, of which 2 were waited for; matrix products, arithmetic and copies ran while one was open for 0% of the time, Pallas kernels for 0%

profile of v2, /device:TPU:0, one launch (start us, length us, event | category | flops | bytes accessed | tf_op | source)
XLA Modules:
  0.0 108.3 jit_solution(438427191459772650)
XLA Ops:
  0.6 2.6 %shard_map.84 = bf16[16,8,4,16,128]{4,3,2,1,0:T(8,128)(2,1)} custom-call(bf16[32,8192]{1,0:T(8,128)(2,1)} %q_hbm.1, bf16[32,8192]{1,0:T(8,128)(2,1)} %g_hbm.1, bf16[32,1024]{1,0:T(8,128)(2,1)} %k_hbm.1, bf16[32,1024]{1,0:T(8,128)(2,1)} %v_hbm.1), custom_call_target="tpu_custom_call" | custom-call | tf_op jit(solution)/shard_map/pallas_call | solution.py:262
  3.2 39.8 %all_to_all.10.got_ref = bf16[128,4,16,128]{3,2,1,0:T(8,128)(2,1)S(1)} all-to-all(bf16[128,4,16,128]{3,2,1,0:T(8,128)(2,1)} %bitcast.2), channel_id=1, replica_groups=mesh['ctx'=16,'tp'=8] {'ctx','tp'}, dimensions={0} | all-to-all | bytes 4194304 | tf_op jit(solution)/shard_map/all_to_all | solution.py:250
  43.1 0.0 copy-start
  43.1 0.1 shard_map.85
  43.2 0.1 collective-permute-start
  43.3 0.5 copy-done
  43.8 0.2 convert_reduce_fusion
  44.0 0.1 pad_add_fusion.info_ref
  44.1 1.9 %collective-permute-done.far_ref = bf16[128,2,16,128]{3,2,1,0:T(8,128)(2,1)} collective-permute-done((bf16[128,2,16,128]{3,2,1,0:T(8,128)(2,1)S(1)}, bf16[128,2,16,128]{3,2,1,0:T(8,128)(2,1)}, u32[]{:S(2)}, u32[]{:S(2)}) %collective-permute-start) | collective-permute-done | bytes 1048608 | tf_op jit(solution)/shard_map/ppermute | solution.py:254
  46.0 23.3 %shard_map.86 = (bf16[128,2,16,128]{3,2,1,0:T(8,128)(2,1)S(1)}, f32[128,2,16,128]{3,2,1,0:T(8,128)S(1)}, bf16[128,2,16,128]{3,2,1,0:T(8,128)(2,1)S(1)}) custom-call(s32[4]{0:T(128)S(1)} %pad_add_fusion.info_ref, bf16[128,4,16,128]{3,2,1,0:T(8,128)(2,1)S(1)} %all_to_all.10.got_ref, bf16[128,2,16,128]{3,2,1,0:T(8,128)(2,1)} %collective-permute-done.far_ref), custom_call_target="tpu_custom_call" | custom-call | tf_op jit(solution)/shard_map/pallas_call | solution.py:288
  69.3 0.2 collective-permute-start.1
  69.6 2.5 %collective-permute-done.1.back_ref = bf16[128,2,16,128]{3,2,1,0:T(8,128)(2,1)S(1)} collective-permute-done((bf16[128,2,16,128]{3,2,1,0:T(8,128)(2,1)S(1)}, bf16[128,2,16,128]{3,2,1,0:T(8,128)(2,1)S(1)}, u32[]{:S(2)}, u32[]{:S(2)}) %collective-permute-start.1) | collective-permute-done | bytes 1048608 | tf_op jit(solution)/shard_map/ppermute | solution.py:254
  72.1 0.3 shard_map.87
  72.3 34.4 %all_to_all.11.got_ref = bf16[128,4,16,128]{3,2,1,0:T(8,128)(2,1)S(1)} all-to-all(bf16[128,4,16,128]{3,2,1,0:T(8,128)(2,1)S(1)} %shard_map.87), channel_id=1, replica_groups=mesh['ctx'=16,'tp'=8] {'ctx','tp'}, dimensions={0} | all-to-all | bytes 4194304 | tf_op jit(solution)/shard_map/all_to_all | solution.py:250
  106.8 1.5 %shard_map.88 = (f32[32,8192]{1,0:T(8,128)}, f32[32,8192]{1,0:T(8,128)}, f32[32,1024]{1,0:T(8,128)}, f32[32,1024]{1,0:T(8,128)}) custom-call(bf16[128,4,16,128]{3,2,1,0:T(8,128)(2,1)S(1)} %all_to_all.11.got_ref), custom_call_target="tpu_custom_call" | custom-call | tf_op jit(solution)/shard_map/pallas_call | solution.py:322
  (1 shorter events, 0.0 us)
Async XLA Ops:
  43.1 0.7 copy-start
  43.2 2.9 %collective-permute-start = (bf16[128,2,16,128]{3,2,1,0:T(8,128)(2,1)S(1)}, bf16[128,2,16,128]{3,2,1,0:T(8,128)(2,1)}, u32[]{:S(2)}, u32[]{:S(2)}) collective-permute-start(bf16[128,2,16,128]{3,2,1,0:T(8,128)(2,1)S(1)} %shard_map.85), channel_id=1, source_target_pairs={{0,8},{8,0},{16,24},{24,16},{32,40},{40,32},{48,56},{56,48},{64,72... | collective-permute-start | bytes 3145736 | tf_op jit(solution)/shard_map/ppermute | solution.py:254
  69.3 2.7 %collective-permute-start.1 = (bf16[128,2,16,128]{3,2,1,0:T(8,128)(2,1)S(1)}, bf16[128,2,16,128]{3,2,1,0:T(8,128)(2,1)S(1)}, u32[]{:S(2)}, u32[]{:S(2)}) collective-permute-start(bf16[128,2,16,128]{3,2,1,0:T(8,128)(2,1)S(1)} %get-tuple-element.9), channel_id=1, source_target_pairs={{0,8},{8,0},{16,24},{24,16},{32,40},{40,32},{48,56},{56,48},{64,72... | collective-permute-start | bytes 3145736 | tf_op jit(solution)/shard_map/ppermute | solution.py:254

commit v3 on v2

v3 whole, which is shorter than its diff:
```python
import math

import jax
import jax.numpy as jnp
from jax import lax
from jax.experimental import pallas as pl
from jax.experimental.pallas import tpu as pltpu
from jax.sharding import PartitionSpec as P

HD = 128
GROUP = 8
KV = 8
DEV = 128
HALF = 16
PIECE = (HALF, HD)
TOKENS = 4096
ROWS = 512
FAR = ROWS
TILE = 256
TILES = range(0, FAR, TILE)
KEYS = 2 * FAR
BLOCKS = TOKENS // KEYS
STEPS = BLOCKS * (BLOCKS + 1) // 2
SPAN = ROWS // HALF
SCALE = HD**-0.5
LOG2E = math.log2(math.e)
VERY_LOW = -1e30
NT = (((1,), (1,)), ((), ()))
MIB = 1 << 20


def mm(a, b):
    return jnp.dot(a, b, preferred_element_type=jnp.float32)


def mm_nt(a, b):
    return lax.dot_general(a, b, NT, preferred_element_type=jnp.float32)


def pack_kernel(q_hbm, g_hbm, k_hbm, v_hbm, out_hbm, q_ref, g_ref, k_ref, v_ref, out_ref, sems):
    arrays = ((q_hbm, q_ref), (g_hbm, g_ref), (k_hbm, k_ref), (v_hbm, v_ref))
    arrived, left = [], []
    for g in range(KV):
        for n, (src, dst) in enumerate(arrays):
            width = src.shape[1] // KV
            columns = pl.ds(g * width, width)
            arrived.append(
                pltpu.make_async_copy(src.at[:, columns], dst.at[:, columns], sems.at[g, n])
            )
            arrived[-1].start()
    for g in range(KV):
        for copy in arrived[4 * g : 4 * g + 4]:
            copy.wait()
        for hh in range(GROUP):
            for s in range(2):
                rows = slice(s * HALF, (s + 1) * HALF)
                head = slice((g * GROUP + hh) * HD, (g * GROUP + hh + 1) * HD)
                group = slice(g * HD, (g + 1) * HD)
                to = hh * 2 + s
                out_ref[to, g, 0] = q_ref[rows, head]
                out_ref[to, g, 1] = g_ref[rows, head]
                out_ref[to, g, 2] = k_ref[rows, group]
                out_ref[to, g, 3] = v_ref[rows, group]
        left.append(pltpu.make_async_copy(out_ref.at[:, g], out_hbm.at[:, g], sems.at[g, 4]))
        left[-1].start()
    for copy in left:
        copy.wait()


def split_kernel(got_ref, own_ref):
    own_ref[...] = got_ref[:, 2:]


def doc_start_in(info_ref):
    first_1, first_2, first_3 = info_ref[0], info_ref[1], info_ref[2]

    def doc_start(token):
        start = jnp.where(token >= first_1, first_1, 0)
        start = jnp.where(token >= first_2, first_2, start)
        return jnp.where(token >= first_3, first_3, start)

    return doc_start


def spread(r):
    return r + (r & ~(HALF - 1))


def step_of(i, j):
    return i * (i + 1) // 2 + j


def score_rows(i, key_half, info_ref, q, keys, put, top):
    doc_start = doc_start_in(info_ref)
    first = i * KEYS
    q_tok = first + HALF * info_ref[3] + spread(lax.broadcasted_iota(jnp.int32, (1, ROWS), 1))
    q_start = doc_start(q_tok)

    def k_token(j, t):
        r = lax.broadcasted_iota(jnp.int32, (TILE, 1), 0)
        return j * KEYS + spread(t + r) + HALF * key_half

    def put_top(s, r0):
        top[:, r0:] = jnp.maximum(
            top[:, r0:], jnp.max(s.reshape(TILE // 8, 8, ROWS - r0), axis=0)
        )

    for t in TILES:
        k_tok = k_token(i, t)
        s = mm_nt(keys(i, t), q[t:])
        s = jnp.where((k_tok <= q_tok[:, t:]) & (k_tok >= q_start[:, t:]), s, VERY_LOW)
        put(i, t, t, s)
        put_top(s, t)

    for j in range(i):
        for t in TILES:
            s = jnp.where(k_token(j, t) >= q_start, mm_nt(keys(j, t), q), VERY_LOW)
            put(j, t, 0, s)
            put_top(s, 0)


def keys_of(ref, which):
    def keys(j, t):
        return ref[pl.ds(j * SPAN + t // HALF, TILE // HALF), which].reshape(TILE, HD)

    return keys


def turn(ref, which, out_ref, j):
    out_ref[j] = ref[pl.ds(j * SPAN, SPAN), which].reshape(FAR, HD).T


def near_kernel(info_ref, got_ref, near_ref, s_near, top_near, k_t, v_t):
    def turns(j, carry):
        turn(near_ref, 0, k_t, j)
        turn(near_ref, 1, v_t, j)
        return carry

    lax.fori_loop(0, BLOCKS, turns, 0)

    def block(i, carry):
        q = got_ref[pl.ds(i * SPAN, SPAN), 0].reshape(ROWS, HD)
        top = top_near.at[i]
        top[...] = jnp.full((8, ROWS), VERY_LOW, jnp.float32)

        def put(j, t, r0, s):
            s_near[step_of(i, j), t : t + TILE, r0:] = s

        score_rows(i, info_ref[3], info_ref, q, keys_of(near_ref, 0), put, top)
        return carry

    for i in range(BLOCKS):
        block(i, 0)


def far_kernel(
    info_ref, got_ref, far_ref, s_near, top_near, v_t_near,
    o_ref, dq_part, stats, oth_ref,
    k_t, v_t, dk_acc, dv_acc, s_far, top, tot, o_t,
):
    def turns(j, carry):
        turn(far_ref, 0, k_t, j)
        turn(far_ref, 1, v_t, j)
        return carry

    lax.fori_loop(0, BLOCKS, turns, 0)
    k_far, v_far = keys_of(far_ref, 0), keys_of(far_ref, 1)

    def rows_of(i, which):
        return got_ref[i * SPAN : (i + 1) * SPAN, which].reshape(ROWS, HD)

    for i in range(BLOCKS):
        top[i] = top_near[i]

        def put(j, t, r0, s):
            s_far[step_of(i, j), t : t + TILE, r0:] = s

        score_rows(i, 1 - info_ref[3], info_ref, rows_of(i, 0), k_far, put, top.at[i])

    for i in range(BLOCKS):
        shift = jnp.max(top[i], axis=0, keepdims=True) * (SCALE * LOG2E)

        def mix_tile(j, t, r0):
            at = step_of(i, j)
            e_near = jnp.exp2(s_near[at, t : t + TILE, r0:] * (SCALE * LOG2E) - shift[:, r0:])
            e_far = jnp.exp2(s_far[at, t : t + TILE, r0:] * (SCALE * LOG2E) - shift[:, r0:])
            s_far[at, t : t + TILE, r0:] = e_far
            e_sum = jnp.sum((e_near + e_far).reshape(TILE // 8, 8, ROWS - r0), axis=0)
            mixed = mm(v_t_near[j, :, t : t + TILE], e_near.astype(jnp.bfloat16))
            return e_sum, mixed + mm(v_t[j, :, t : t + TILE], e_far.astype(jnp.bfloat16))

        for t in TILES:
            e_sum, mixed = mix_tile(i, t, t)
            tot[i, :, t:] = e_sum if t == 0 else tot[i, :, t:] + e_sum
            o_t[i, :, t:] = mixed if t == 0 else o_t[i, :, t:] + mixed
        for j in range(i):
            for t in TILES:
                e_sum, mixed = mix_tile(j, t, 0)
                tot[i] += e_sum
                o_t[i] += mixed

    for i in range(BLOCKS):
        span = slice(i * SPAN, (i + 1) * SPAN)
        shift = jnp.max(top[i], axis=0, keepdims=True) * (SCALE * LOG2E)
        total = jnp.sum(tot[i], axis=0, keepdims=True)
        inverse = 1.0 / total
        out_t = o_t[i] * inverse
        o_ref[span] = out_t.T.astype(jnp.bfloat16).reshape(SPAN, *PIECE)
        delta = jnp.sum(rows_of(i, 1).T.astype(jnp.float32) * out_t, axis=0, keepdims=True)
        stats[i, 0] = jnp.broadcast_to(shift + jnp.log(total) * LOG2E, (8, ROWS))
        stats[i, 1] = jnp.broadcast_to(delta, (8, ROWS))
        tot[i] = jnp.broadcast_to(inverse, (8, ROWS))

    for i in range(BLOCKS):
        q, g = rows_of(i, 0), rows_of(i, 1)
        inverse = tot[i, :1]
        delta = stats[i, 1, :1]

        def back_tile(j, t, r0):
            prob = s_far[step_of(i, j), t : t + TILE, r0:] * inverse[:, r0:]
            d_prob = mm_nt(v_far(j, t), g[r0:])
            d_score = (prob * (d_prob - delta[:, r0:])).astype(jnp.bfloat16)
            return (
                mm(prob.astype(jnp.bfloat16), g[r0:]),
                mm(d_score, q[r0:]),
                mm(k_t[j, :, t : t + TILE], d_score),
            )

        back_rows(i, back_tile, dv_acc, dk_acc, dq_part.at[i])

    def give(j, carry):
        span = pl.ds(j * SPAN, SPAN)
        oth_ref[span, 0] = (dk_acc[j] * SCALE).astype(jnp.bfloat16).reshape(SPAN, *PIECE)
        oth_ref[span, 1] = dv_acc[j].astype(jnp.bfloat16).reshape(SPAN, *PIECE)
        return carry

    lax.fori_loop(0, BLOCKS, give, 0)


def back_rows(i, back_tile, dv_acc, dk_acc, dq_t):
    for t in TILES:
        dv, dk, dq = back_tile(i, t, t)
        dv_acc[i, t : t + TILE] = dv
        dk_acc[i, t : t + TILE] = dk
        dq_t[:, t:] = dq if t == 0 else dq_t[:, t:] + dq

    for j in range(i):
        for t in TILES:
            dv, dk, dq = back_tile(j, t, 0)
            dv_acc[j, t : t + TILE] += dv
            dk_acc[j, t : t + TILE] += dk
            dq_t[...] += dq


def own_kernel(
    got_ref, near_ref, s_near, k_t, stats, dq_part,
    dq_ref, own_ref,
    dk_acc, dv_acc, dq_t,
):
    v_near = keys_of(near_ref, 1)

    def block(i, carry):
        span = pl.ds(i * SPAN, SPAN)
        q = got_ref[span, 0].reshape(ROWS, HD)
        g = got_ref[span, 1].reshape(ROWS, HD)
        log_total = stats[i, 0, :1]
        delta = stats[i, 1, :1]

        def back_tile(j, t, r0):
            s = s_near[step_of(i, j), t : t + TILE, r0:]
            prob = jnp.exp2(s * (SCALE * LOG2E) - log_total[:, r0:])
            d_prob = mm_nt(v_near(j, t), g[r0:])
            d_score = (prob * (d_prob - delta[:, r0:])).astype(jnp.bfloat16)
            return (
                mm(prob.astype(jnp.bfloat16), g[r0:]),
                mm(d_score, q[r0:]),
                mm(k_t[j, :, t : t + TILE], d_score),
            )

        back_rows(i, back_tile, dv_acc, dk_acc, dq_t)
        dq = (dq_t[...] + dq_part[i]) * SCALE
        dq_ref[span] = dq.T.astype(jnp.bfloat16).reshape(SPAN, *PIECE)
        return carry

    for i in range(BLOCKS):
        block(i, 0)

    def give(j, carry):
        span = pl.ds(j * SPAN, SPAN)
        own_ref[span, 0] = (dk_acc[j] * SCALE).reshape(SPAN, *PIECE)
        own_ref[span, 1] = dv_acc[j].reshape(SPAN, *PIECE)
        return carry

    lax.fori_loop(0, BLOCKS, give, 0)


def join_kernel(o_ref, dq_ref, own_ref, back_ref, out_ref):
    out_ref[:, 0] = o_ref[...]
    out_ref[:, 1] = dq_ref[...]
    out_ref[:, 2:] = (own_ref[...] + back_ref[...].astype(jnp.float32)).astype(jnp.bfloat16)


def unpack_kernel(got_ref, o_hbm, dq_hbm, dk_hbm, dv_hbm, o_ref, dq_ref, dk_ref, dv_ref, sems):
    copies = []

    def send(src, dst):
        copies.append(pltpu.make_async_copy(src, dst, sems.at[len(copies)]))
        copies[-1].start()

    for g in range(KV):
        group = slice(g * HD, (g + 1) * HD)
        for s in range(2):
            rows = slice(s * HALF, (s + 1) * HALF)
            dk = jnp.zeros(PIECE, jnp.float32)
            dv = jnp.zeros(PIECE, jnp.float32)
            for hh in range(GROUP):
                at = (hh * 2 + s) * KV + g
                head = slice((g * GROUP + hh) * HD, (g * GROUP + hh + 1) * HD)
                o_ref[rows, head] = got_ref[at, 0].astype(jnp.float32)
                dq_ref[rows, head] = got_ref[at, 1].astype(jnp.float32)
                dk += got_ref[at, 2].astype(jnp.float32)
                dv += got_ref[at, 3].astype(jnp.float32)
            dk_ref[rows, group] = dk
            dv_ref[rows, group] = dv
        heads = pl.ds(g * GROUP * HD, GROUP * HD)
        send(o_ref.at[:, heads], o_hbm.at[:, heads])
        send(dq_ref.at[:, heads], dq_hbm.at[:, heads])
    send(dk_ref, dk_hbm)
    send(dv_ref, dv_hbm)
    for copy in copies:
        copy.wait()


def everyone(x):
    return lax.all_to_all(x, ("ctx", "tp"), 0, 0, tiled=True)


def swap_cores(x):
    return lax.ppermute(x, "ctx", [(c, c ^ 1) for c in range(16)])


def per_device(queries, keys, values, out_grad, doc_ids):
    bf16, f32 = jnp.bfloat16, jnp.float32
    wide, narrow = (2 * HALF, KV * GROUP * HD), (2 * HALF, KV * HD)
    hbm = pl.BlockSpec(memory_space=pltpu.HBM)
    packed = (DEV // KV, KV, 4, *PIECE)
    sent = pl.pallas_call(
        pack_kernel,
        out_shape=jax.ShapeDtypeStruct(packed, bf16),
        in_specs=[hbm] * 4,
        out_specs=hbm,
        scratch_shapes=[
            pltpu.VMEM(wide, bf16),
            pltpu.VMEM(wide, bf16),
            pltpu.VMEM(narrow, bf16),
            pltpu.VMEM(narrow, bf16),
            pltpu.VMEM(packed, bf16),
            pltpu.SemaphoreType.DMA((KV, 5)),
        ],
        compiler_params=pltpu.CompilerParams(vmem_limit_bytes=60 * MIB),
    )(queries, out_grad, keys, values).reshape(DEV, 4, *PIECE)
    got = everyone(sent)
    pair = (DEV, 2, *PIECE)
    near = pl.pallas_call(
        split_kernel,
        out_shape=jax.ShapeDtypeStruct(pair, bf16),
        compiler_params=pltpu.CompilerParams(vmem_limit_bytes=16 * MIB),
    )(got)
    far = swap_cores(near)
    firsts = jnp.sum(doc_ids[None, :] < jnp.arange(1, 4, dtype=jnp.int32)[:, None], axis=1)
    half = lax.axis_index("ctx") % 2
    info = jnp.concatenate([firsts.astype(jnp.int32), half.astype(jnp.int32)[None]])
    smem = pl.BlockSpec(memory_space=pltpu.SMEM)
    vmem = pl.BlockSpec(memory_space=pltpu.VMEM)

    def out(shape, dtype):
        return jax.ShapeDtypeStruct(shape, dtype)

    def cost(flops):
        return pl.CostEstimate(flops=int(flops), bytes_accessed=MIB, transcendentals=0)

    single = (DEV, *PIECE)
    turned = (BLOCKS, HD, FAR)
    s_near, top_near, k_t, v_t = pl.pallas_call(
        near_kernel,
        out_shape=(
            out((STEPS, FAR, ROWS), f32),
            out((BLOCKS, 8, ROWS), f32),
            out(turned, bf16),
            out(turned, bf16),
        ),
        in_specs=[smem, vmem, vmem],
        compiler_params=pltpu.CompilerParams(vmem_limit_bytes=24 * MIB),
        cost_estimate=cost(4e9),
    )(info, got, near)
    o, dq_part, stats, oth = pl.pallas_call(
        far_kernel,
        out_shape=(
            out(single, bf16),
            out((BLOCKS, HD, ROWS), f32),
            out((BLOCKS, 2, 8, ROWS), f32),
            out(pair, bf16),
        ),
        in_specs=[smem] + [vmem] * 5,
        scratch_shapes=[
            pltpu.VMEM(turned, bf16),
            pltpu.VMEM(turned, bf16),
            pltpu.VMEM((BLOCKS, FAR, HD), f32),
            pltpu.VMEM((BLOCKS, FAR, HD), f32),
            pltpu.VMEM((STEPS, FAR, ROWS), f32),
            pltpu.VMEM((BLOCKS, 8, ROWS), f32),
            pltpu.VMEM((BLOCKS, 8, ROWS), f32),
            pltpu.VMEM((BLOCKS, HD, ROWS), f32),
        ],
        compiler_params=pltpu.CompilerParams(vmem_limit_bytes=32 * MIB),
        cost_estimate=cost(16e9),
    )(info, got, far, s_near, top_near, v_t)
    back = swap_cores(oth)
    dq, own = pl.pallas_call(
        own_kernel,
        out_shape=(out(single, bf16), out(pair, f32)),
        in_specs=[vmem] * 6,
        scratch_shapes=[
            pltpu.VMEM((BLOCKS, FAR, HD), f32),
            pltpu.VMEM((BLOCKS, FAR, HD), f32),
            pltpu.VMEM((HD, ROWS), f32),
        ],
        compiler_params=pltpu.CompilerParams(vmem_limit_bytes=28 * MIB),
        cost_estimate=cost(8e9),
    )(got, near, s_near, k_t, stats, dq_part)
    returned = everyone(
        pl.pallas_call(
            join_kernel,
            out_shape=out((DEV, 4, *PIECE), bf16),
            compiler_params=pltpu.CompilerParams(vmem_limit_bytes=16 * MIB),
        )(o, dq, own, back)
    )
    return pl.pallas_call(
        unpack_kernel,
        out_shape=(
            jax.ShapeDtypeStruct(wide, f32),
            jax.ShapeDtypeStruct(wide, f32),
            jax.ShapeDtypeStruct(narrow, f32),
            jax.ShapeDtypeStruct(narrow, f32),
        ),
        out_specs=[hbm] * 4,
        scratch_shapes=[
            pltpu.VMEM(wide, f32),
            pltpu.VMEM(wide, f32),
            pltpu.VMEM(narrow, f32),
            pltpu.VMEM(narrow, f32),
            pltpu.SemaphoreType.DMA((2 * KV + 2,)),
        ],
        compiler_params=pltpu.CompilerParams(vmem_limit_bytes=16 * MIB),
    )(returned)


def solution(mesh):
    rows = P(("ctx", "tp"), None)
    return jax.shard_map(
        per_device,
        mesh=mesh,
        in_specs=(rows, rows, rows, rows, P()),
        out_specs=(rows, rows, rows, rows),
        check_vma=False,
    )
```

time: 109 us -> 103 us (0.945)
  waiting for transfers between devices: 4.44 us -> 0.01 us
  Pallas kernels: 27.8 us -> 25.1 us
    ppermute x2, waiting for transfers between devices: 4.44 us -> 0.01 us  [swap_cores(): return lax.ppermute(x, 'ctx', [(c, c ^ 1) for c in range(16)])]
    pallas_call x2 -> x4, Pallas kernels: 23.5 us -> 20.9 us  [the longest x1 12.7 us: per_device(): pl.pallas_call(far_kernel, out_shape=(out(single, bf16), out((BLOCKS, HD,...]
  transfers between devices with their start and end apart: 2 -> 2, of which waited for: 2 -> 0; matrix products, arithmetic and copies ran while one was open for 0% -> 0% of each run, Pallas kernels for 0% -> 8%
where the time goes in v3:
time: 103 us; the launch traced here: 102 us
  blocking collectives  74.4 us (72%)
  Pallas kernels  25.1 us (24%)
    all_to_all x2, blocking collectives, everyone(): return lax.all_to_all(x, ('ctx', 'tp'), 0, 0, tiled=True)  74.4 us
    pallas_call x1, Pallas kernels, per_device(): pl.pallas_call(far_kernel, out_shape=(out(single, bf16), out((BLOCKS, HD,...  12.7 us
    pallas_call x1, Pallas kernels, per_device(): pl.pallas_call(own_kernel, out_shape=(out(single, bf16), out(pair, f32)),...  5.16 us
    pallas_call x1, Pallas kernels, per_device(): pl.pallas_call(near_kernel, out_shape=(out((STEPS, FAR, ROWS), f32), out(...  2.66 us
    pallas_call x1, Pallas kernels, per_device(): pl.pallas_call(pack_kernel, out_shape=jax.ShapeDtypeStruct(packed, bf16),...  2.62 us
  transfers between devices with their start and end apart: 2, of which 0 were waited for; matrix products, arithmetic and copies ran while one was open for 0% of the time, Pallas kernels for 8%

profile of v3, /device:TPU:0, one launch (start us, length us, event | category | flops | bytes accessed | tf_op | source)
XLA Modules:
  0.0 101.6 jit_solution(17888381753658065289)
XLA Ops:
  0.6 2.6 %shard_map.84 = bf16[16,8,4,16,128]{4,3,2,1,0:T(8,128)(2,1)} custom-call(bf16[32,8192]{1,0:T(8,128)(2,1)} %q_hbm.1, bf16[32,8192]{1,0:T(8,128)(2,1)} %g_hbm.1, bf16[32,1024]{1,0:T(8,128)(2,1)} %k_hbm.1, bf16[32,1024]{1,0:T(8,128)(2,1)} %v_hbm.1), custom_call_target="tpu_custom_call" | custom-call | tf_op jit(solution)/shard_map/pallas_call | solution.py:347
  3.3 39.8 %all_to_all.10.got_ref = bf16[128,4,16,128]{3,2,1,0:T(8,128)(2,1)S(1)} all-to-all(bf16[128,4,16,128]{3,2,1,0:T(8,128)(2,1)} %bitcast.2), channel_id=1, replica_groups=mesh['ctx'=16,'tp'=8] {'ctx','tp'}, dimensions={0} | all-to-all | bytes 4194304 | tf_op jit(solution)/shard_map/all_to_all | solution.py:335
  43.1 0.0 copy-start
  43.1 0.1 shard_map.85.near_ref
  43.2 0.1 collective-permute-start
  43.3 0.5 copy-done
  43.8 0.2 convert_reduce_fusion
  44.0 0.1 pad_add_fusion.info_ref
  44.1 2.7 %shard_map.86 = (f32[10,512,512]{2,1,0:T(8,128)S(1)}, f32[4,8,512]{2,1,0:T(8,128)S(1)}, bf16[4,128,512]{2,1,0:T(8,128)(2,1)S(1)}, bf16[4,128,512]{2,1,0:T(8,128)(2,1)S(1)}) custom-call(s32[4]{0:T(128)S(1)} %pad_add_fusion.info_ref, bf16[128,4,16,128]{3,2,1,0:T(8,128)(2,1)S(1)} %all_to_all.10.got_ref, bf16[128,2,16,128]{3,2,1,0:T(8,128)(2,1)S(1)} %shard_map.85.near_ref), custom_call_target="tpu_custom_call" | custom-call | flops 4000000000 | bytes 1048576 | tf_op jit(solution)/shard_map/pallas_call | solution.py:384
  46.8 0.0 collective-permute-done.far_ref
  46.8 12.7 %shard_map.87 = (bf16[128,16,128]{2,1,0:T(8,128)(2,1)S(1)}, f32[4,128,512]{2,1,0:T(8,128)S(1)}, f32[4,2,8,512]{3,2,1,0:T(8,128)S(1)}, bf16[128,2,16,128]{3,2,1,0:T(8,128)(2,1)S(1)}) custom-call(s32[4]{0:T(128)S(1)} %pad_add_fusion.info_ref, bf16[128,4,16,128]{3,2,1,0:T(8,128)(2,1)S(1)} %all_to_all.10.got_ref, ...), custom_call_target="tpu_custom_call" | custom-call | flops 16000000000 | bytes 1048576 | tf_op jit(solution)/shard_map/pallas_call | solution.py:396
  59.5 0.3 collective-permute-start.1
  59.8 5.2 %shard_map.88 = (bf16[128,16,128]{2,1,0:T(8,128)(2,1)S(1)}, f32[128,2,16,128]{3,2,1,0:T(8,128)S(1)}) custom-call(bf16[128,4,16,128]{3,2,1,0:T(8,128)(2,1)S(1)} %all_to_all.10.got_ref, bf16[128,2,16,128]{3,2,1,0:T(8,128)(2,1)S(1)} %shard_map.85.near_ref, f32[10,512,512]{2,1,0:T(8,128)S(1)} %get-tuple-element.14.s_near, ...), custom_call_target="tpu_custom_call" | custom-call | flops 8000000000 | bytes 1048576 | tf_op jit(solution)/shard_map/pallas_call | solution.py:419
  65.0 0.0 collective-permute-done.1.back_ref
  65.0 0.3 shard_map.89
  65.3 34.5 %all_to_all.11.got_ref = bf16[128,4,16,128]{3,2,1,0:T(8,128)(2,1)S(1)} all-to-all(bf16[128,4,16,128]{3,2,1,0:T(8,128)(2,1)S(1)} %shard_map.89), channel_id=1, replica_groups=mesh['ctx'=16,'tp'=8] {'ctx','tp'}, dimensions={0} | all-to-all | bytes 4194304 | tf_op jit(solution)/shard_map/all_to_all | solution.py:335
  99.9 1.5 %shard_map.90 = (f32[32,8192]{1,0:T(8,128)}, f32[32,8192]{1,0:T(8,128)}, f32[32,1024]{1,0:T(8,128)}, f32[32,1024]{1,0:T(8,128)}) custom-call(bf16[128,4,16,128]{3,2,1,0:T(8,128)(2,1)S(1)} %all_to_all.11.got_ref), custom_call_target="tpu_custom_call" | custom-call | tf_op jit(solution)/shard_map/pallas_call | solution.py:438
  (1 shorter events, 0.0 us)
Async XLA Ops:
  43.1 0.7 copy-start
  43.2 3.6 %collective-permute-start = (bf16[128,2,16,128]{3,2,1,0:T(8,128)(2,1)S(1)}, bf16[128,2,16,128]{3,2,1,0:T(8,128)(2,1)}, u32[]{:S(2)}, u32[]{:S(2)}) collective-permute-start(bf16[128,2,16,128]{3,2,1,0:T(8,128)(2,1)S(1)} %shard_map.85.near_ref), channel_id=1, source_target_pairs={{0,8},{8,0},{16,24},{24,16},{32,40},{40,32},{48,56},{56,48},{64,72... | collective-permute-start | bytes 3145736 | tf_op jit(solution)/shard_map/ppermute | solution.py:339
  59.5 5.5 %collective-permute-start.1 = (bf16[128,2,16,128]{3,2,1,0:T(8,128)(2,1)S(1)}, bf16[128,2,16,128]{3,2,1,0:T(8,128)(2,1)S(1)}, u32[]{:S(2)}, u32[]{:S(2)}) collective-permute-start(bf16[128,2,16,128]{3,2,1,0:T(8,128)(2,1)S(1)} %get-tuple-element.23), channel_id=1, source_target_pairs={{0,8},{8,0},{16,24},{24,16},{32,40},{40,32},{48,56},{56,48},{64,72... | collective-permute-start | bytes 3145736 | tf_op jit(solution)/shard_map/ppermute | solution.py:339

commit v4 on v3

--- a/solution.py
+++ b/solution.py
@@ -1,3 +1,4 @@
+import functools
 import math
 
 import jax
@@ -11,8 +12,8 @@
 GROUP = 8
 KV = 8
 DEV = 128
-HALF = 16
-PIECE = (HALF, HD)
+OWN = 16
+PIECE = (OWN, HD)
 TOKENS = 4096
 ROWS = 512
 FAR = ROWS
@@ -21,7 +22,7 @@
 KEYS = 2 * FAR
 BLOCKS = TOKENS // KEYS
 STEPS = BLOCKS * (BLOCKS + 1) // 2
-SPAN = ROWS // HALF
+SPAN = ROWS // OWN
 SCALE = HD**-0.5
 LOG2E = math.log2(math.e)
 VERY_LOW = -1e30
@@ -53,7 +54,7 @@
             copy.wait()
         for hh in range(GROUP):
             for s in range(2):
-                rows = slice(s * HALF, (s + 1) * HALF)
+                rows = slice(s * OWN, (s + 1) * OWN)
                 head = slice((g * GROUP + hh) * HD, (g * GROUP + hh + 1) * HD)
                 group = slice(g * HD, (g + 1) * HD)
                 to = hh * 2 + s
@@ -83,45 +84,59 @@
 
 
 def spread(r):
-    return r + (r & ~(HALF - 1))
+    return r + (r & ~(OWN - 1))
 
 
 def step_of(i, j):
     return i * (i + 1) // 2 + j
 
 
-def score_rows(i, key_half, info_ref, q, keys, put, top):
+def score_tiles(i, key_half, info_ref, q, keys, put, top):
     doc_start = doc_start_in(info_ref)
     first = i * KEYS
-    q_tok = first + HALF * info_ref[3] + spread(lax.broadcasted_iota(jnp.int32, (1, ROWS), 1))
+    q_tok = first + OWN * info_ref[3] + spread(lax.broadcasted_iota(jnp.int32, (1, ROWS), 1))
     q_start = doc_start(q_tok)
 
     def k_token(j, t):
         r = lax.broadcasted_iota(jnp.int32, (TILE, 1), 0)
-        return j * KEYS + spread(t + r) + HALF * key_half
+        return j * KEYS + spread(t + r) + OWN * key_half
 
     def put_top(s, r0):
         top[:, r0:] = jnp.maximum(
             top[:, r0:], jnp.max(s.reshape(TILE // 8, 8, ROWS - r0), axis=0)
         )
 
-    for t in TILES:
+    def diagonal(t):
         k_tok = k_token(i, t)
         s = mm_nt(keys(i, t), q[t:])
         s = jnp.where((k_tok <= q_tok[:, t:]) & (k_tok >= q_start[:, t:]), s, VERY_LOW)
         put(i, t, t, s)
         put_top(s, t)
 
-    for j in range(i):
-        for t in TILES:
-            s = jnp.where(k_token(j, t) >= q_start, mm_nt(keys(j, t), q), VERY_LOW)
-            put(j, t, 0, s)
-            put_top(s, 0)
+    def full(j, t):
+        s = jnp.where(k_token(j, t) >= q_start, mm_nt(keys(j, t), q), VERY_LOW)
+        put(j, t, 0, s)
+        put_top(s, 0)
+
+    return [functools.partial(diagonal, t) for t in TILES] + [
+        functools.partial(full, j, t) for j in range(i) for t in TILES
+    ]
+
+
+def run(steps):
+    for step in steps:
+        step()
+
+
+def beside(one, other):
+    placed = [((n + 0.5) / len(steps), k, step) for k, steps in enumerate((one, other))
+              for n, step in enumerate(steps)]
+    return [step for _, _, step in sorted(placed, key=lambda item: item[:2])]
 
 
 def keys_of(ref, which):
     def keys(j, t):
-        return ref[pl.ds(j * SPAN + t // HALF, TILE // HALF), which].reshape(TILE, HD)
+        return ref[pl.ds(j * SPAN + t // OWN, TILE // OWN), which].reshape(TILE, HD)
 
     return keys
 
@@ -146,7 +161,7 @@
         def put(j, t, r0, s):
             s_near[step_of(i, j), t : t + TILE, r0:] = s
 
-        score_rows(i, info_ref[3], info_ref, q, keys_of(near_ref, 0), put, top)
+        run(score_tiles(i, info_ref[3], info_ref, q, keys_of(near_ref, 0), put, top))
         return carry
 
     for i in range(BLOCKS):
@@ -154,79 +169,87 @@
 
 
 def far_kernel(
-    info_ref, got_ref, far_ref, s_near, top_near, v_t_near,
+    info_ref, got_ref, far_hbm, s_near, top_near, v_t_near,
     o_ref, dq_part, stats, oth_ref,
-    k_t, v_t, dk_acc, dv_acc, s_far, top, tot, o_t,
+    far_ref, k_t, v_t, dk_acc, dv_acc, s_far, top, tot, o_t, sems,
 ):
-    def turns(j, carry):
-        turn(far_ref, 0, k_t, j)
-        turn(far_ref, 1, v_t, j)
-        return carry
-
-    lax.fori_loop(0, BLOCKS, turns, 0)
+    arriving = []
+    for j in range(BLOCKS):
+        span = pl.ds(j * SPAN, SPAN)
+        arriving.append(pltpu.make_async_copy(far_hbm.at[span], far_ref.at[span], sems.at[j]))
+        arriving[-1].start()
     k_far, v_far = keys_of(far_ref, 0), keys_of(far_ref, 1)
 
     def rows_of(i, which):
         return got_ref[i * SPAN : (i + 1) * SPAN, which].reshape(ROWS, HD)
 
-    for i in range(BLOCKS):
-        top[i] = top_near[i]
-
+    def scores(i):
         def put(j, t, r0, s):
             s_far[step_of(i, j), t : t + TILE, r0:] = s
 
-        score_rows(i, 1 - info_ref[3], info_ref, rows_of(i, 0), k_far, put, top.at[i])
-
-    for i in range(BLOCKS):
-        shift = jnp.max(top[i], axis=0, keepdims=True) * (SCALE * LOG2E)
-
-        def mix_tile(j, t, r0):
+        def begin():
+            arriving[i].wait()
+            top[i] = top_near[i]
+
+        def end():
+            turn(far_ref, 0, k_t, i)
+            turn(far_ref, 1, v_t, i)
+
+        tiles = score_tiles(i, 1 - info_ref[3], info_ref, rows_of(i, 0), k_far, put, top.at[i])
+        return [begin, *tiles, end]
+
+    def mixes(i):
+        def shift():
+            return jnp.max(top[i], axis=0, keepdims=True) * (SCALE * LOG2E)
+
+        def tile(j, t, r0):
             at = step_of(i, j)
-            e_near = jnp.exp2(s_near[at, t : t + TILE, r0:] * (SCALE * LOG2E) - shift[:, r0:])
-            e_far = jnp.exp2(s_far[at, t : t + TILE, r0:] * (SCALE * LOG2E) - shift[:, r0:])
+            e_near = jnp.exp2(s_near[at, t : t + TILE, r0:] * (SCALE * LOG2E) - shift()[:, r0:])
+            e_far = jnp.exp2(s_far[at, t : t + TILE, r0:] * (SCALE * LOG2E) - shift()[:, r0:])
             s_far[at, t : t + TILE, r0:] = e_far
             e_sum = jnp.sum((e_near + e_far).reshape(TILE // 8, 8, ROWS - r0), axis=0)
             mixed = mm(v_t_near[j, :, t : t + TILE], e_near.astype(jnp.bfloat16))
-            return e_sum, mixed + mm(v_t[j, :, t : t + TILE], e_far.astype(jnp.bfloat16))
-
-        for t in TILES:
-            e_sum, mixed = mix_tile(i, t, t)
-            tot[i, :, t:] = e_sum if t == 0 else tot[i, :, t:] + e_sum
-            o_t[i, :, t:] = mixed if t == 0 else o_t[i, :, t:] + mixed
-        for j in range(i):
-            for t in TILES:
-                e_sum, mixed = mix_tile(j, t, 0)
-                tot[i] += e_sum
-                o_t[i] += mixed
-
-    for i in range(BLOCKS):
-        span = slice(i * SPAN, (i + 1) * SPAN)
-        shift = jnp.max(top[i], axis=0, keepdims=True) * (SCALE * LOG2E)
-        total = jnp.sum(tot[i], axis=0, keepdims=True)
-        inverse = 1.0 / total
-        out_t = o_t[i] * inverse
-        o_ref[span] = out_t.T.astype(jnp.bfloat16).reshape(SPAN, *PIECE)
-        delta = jnp.sum(rows_of(i, 1).T.astype(jnp.float32) * out_t, axis=0, keepdims=True)
-        stats[i, 0] = jnp.broadcast_to(shift + jnp.log(total) * LOG2E, (8, ROWS))
-        stats[i, 1] = jnp.broadcast_to(delta, (8, ROWS))
-        tot[i] = jnp.broadcast_to(inverse, (8, ROWS))
-
-    for i in range(BLOCKS):
-        q, g = rows_of(i, 0), rows_of(i, 1)
-        inverse = tot[i, :1]
-        delta = stats[i, 1, :1]
-
-        def back_tile(j, t, r0):
-            prob = s_far[step_of(i, j), t : t + TILE, r0:] * inverse[:, r0:]
+            mixed += mm(v_t[j, :, t : t + TILE], e_far.astype(jnp.bfloat16))
+            new = j == i and t == 0
+            tot[i, :, r0:] = e_sum if new else tot[i, :, r0:] + e_sum
+            o_t[i, :, r0:] = mixed if new else o_t[i, :, r0:] + mixed
+
+        def end():
+            span = slice(i * SPAN, (i + 1) * SPAN)
+            total = jnp.sum(tot[i], axis=0, keepdims=True)
+            inverse = 1.0 / total
+            out_t = o_t[i] * inverse
+            o_ref[span] = out_t.T.astype(jnp.bfloat16).reshape(SPAN, *PIECE)
+            delta = jnp.sum(rows_of(i, 1).T.astype(jnp.float32) * out_t, axis=0, keepdims=True)
+            stats[i, 0] = jnp.broadcast_to(shift() + jnp.log(total) * LOG2E, (8, ROWS))
+            stats[i, 1] = jnp.broadcast_to(delta, (8, ROWS))
+            tot[i] = jnp.broadcast_to(inverse, (8, ROWS))
+
+        return [
+            *(functools.partial(tile, i, t, t) for t in TILES),
+            *(functools.partial(tile, j, t, 0) for j in range(i) for t in TILES),
+            end,
+        ]
+
+    def backs(i):
+        def tile(j, t, r0):
+            q, g = rows_of(i, 0), rows_of(i, 1)
+            prob = s_far[step_of(i, j), t : t + TILE, r0:] * tot[i, :1, r0:]
             d_prob = mm_nt(v_far(j, t), g[r0:])
-            d_score = (prob * (d_prob - delta[:, r0:])).astype(jnp.bfloat16)
+            d_score = (prob * (d_prob - stats[i, 1, :1, r0:])).astype(jnp.bfloat16)
             return (
                 mm(prob.astype(jnp.bfloat16), g[r0:]),
                 mm(d_score, q[r0:]),
                 mm(k_t[j, :, t : t + TILE], d_score),
             )
 
-        back_rows(i, back_tile, dv_acc, dk_acc, dq_part.at[i])
+        return back_tiles(i, tile, dv_acc, dk_acc, dq_part.at[i])
+
+    run(scores(0) + scores(1))
+    run(beside(mixes(0) + mixes(1), scores(2)))
+    run(beside(mixes(2), scores(3)))
+    run(beside(mixes(3), backs(0) + backs(1) + backs(2)))
+    run(backs(3))
 
     def give(j, carry):
         span = pl.ds(j * SPAN, SPAN)
@@ -237,19 +260,22 @@
     lax.fori_loop(0, BLOCKS, give, 0)
 
 
-def back_rows(i, back_tile, dv_acc, dk_acc, dq_t):
-    for t in TILES:
+def back_tiles(i, back_tile, dv_acc, dk_acc, dq_t):
+    def diagonal(t):
         dv, dk, dq = back_tile(i, t, t)
         dv_acc[i, t : t + TILE] = dv
         dk_acc[i, t : t + TILE] = dk
         dq_t[:, t:] = dq if t == 0 else dq_t[:, t:] + dq
 
-    for j in range(i):
-        for t in TILES:
-            dv, dk, dq = back_tile(j, t, 0)
-            dv_acc[j, t : t + TILE] += dv
-            dk_acc[j, t : t + TILE] += dk
-            dq_t[...] += dq
+    def full(j, t):
+        dv, dk, dq = back_tile(j, t, 0)
+        dv_acc[j, t : t + TILE] += dv
+        dk_acc[j, t : t + TILE] += dk
+        dq_t[...] += dq
+
+    return [functools.partial(diagonal, t) for t in TILES] + [
+        functools.partial(full, j, t) for j in range(i) for t in TILES
+    ]
 
 
 def own_kernel(
@@ -277,7 +303,7 @@
                 mm(k_t[j, :, t : t + TILE], d_score),
             )
 
-        back_rows(i, back_tile, dv_acc, dk_acc, dq_t)
+        run(back_tiles(i, back_tile, dv_acc, dk_acc, dq_t))
         dq = (dq_t[...] + dq_part[i]) * SCALE
         dq_ref[span] = dq.T.astype(jnp.bfloat16).reshape(SPAN, *PIECE)
         return carry
@@ -310,7 +336,7 @@
     for g in range(KV):
         group = slice(g * HD, (g + 1) * HD)
         for s in range(2):
-            rows = slice(s * HALF, (s + 1) * HALF)
+            rows = slice(s * OWN, (s + 1) * OWN)
             dk = jnp.zeros(PIECE, jnp.float32)
             dv = jnp.zeros(PIECE, jnp.float32)
             for hh in range(GROUP):
@@ -341,7 +367,7 @@
 
 def per_device(queries, keys, values, out_grad, doc_ids):
     bf16, f32 = jnp.bfloat16, jnp.float32
-    wide, narrow = (2 * HALF, KV * GROUP * HD), (2 * HALF, KV * HD)
+    wide, narrow = (2 * OWN, KV * GROUP * HD), (2 * OWN, KV * HD)
     hbm = pl.BlockSpec(memory_space=pltpu.HBM)
     packed = (DEV // KV, KV, 4, *PIECE)
     sent = pl.pallas_call(
@@ -401,8 +427,9 @@
             out((BLOCKS, 2, 8, ROWS), f32),
             out(pair, bf16),
         ),
-        in_specs=[smem] + [vmem] * 5,
+        in_specs=[smem, vmem, hbm] + [vmem] * 3,
         scratch_shapes=[
+            pltpu.VMEM(pair, bf16),
             pltpu.VMEM(turned, bf16),
             pltpu.VMEM(turned, bf16),
             pltpu.VMEM((BLOCKS, FAR, HD), f32),
@@ -411,6 +438,7 @@
             pltpu.VMEM((BLOCKS, 8, ROWS), f32),
             pltpu.VMEM((BLOCKS, 8, ROWS), f32),
             pltpu.VMEM((BLOCKS, HD, ROWS), f32),
+            pltpu.SemaphoreType.DMA((BLOCKS,)),
         ],
         compiler_params=pltpu.CompilerParams(vmem_limit_bytes=32 * MIB),
         cost_estimate=cost(16e9),

time: 103 us -> 102 us (level)
  no operation moved by 1% of the time
where the time goes in v4:
time: 102 us; the launch traced here: 101 us
  blocking collectives  74.4 us (73%)
  Pallas kernels  24.3 us (24%)
    all_to_all x2, blocking collectives, everyone(): return lax.all_to_all(x, ('ctx', 'tp'), 0, 0, tiled=True)  74.4 us
    pallas_call x1, Pallas kernels, per_device(): pl.pallas_call(far_kernel, out_shape=(out(single, bf16), out((BLOCKS, HD,...  12 us
    pallas_call x1, Pallas kernels, per_device(): pl.pallas_call(own_kernel, out_shape=(out(single, bf16), out(pair, f32)),...  5.16 us
    pallas_call x1, Pallas kernels, per_device(): pl.pallas_call(near_kernel, out_shape=(out((STEPS, FAR, ROWS), f32), out(...  2.66 us
    pallas_call x1, Pallas kernels, per_device(): pl.pallas_call(pack_kernel, out_shape=jax.ShapeDtypeStruct(packed, bf16),...  2.62 us
  transfers between devices with their start and end apart: 2, of which 0 were waited for; matrix products, arithmetic and copies ran while one was open for 0% of the time, Pallas kernels for 8%

profile of v4, /device:TPU:0, one launch (start us, length us, event | category | flops | bytes accessed | tf_op | source)
XLA Modules:
  0.0 100.8 jit_solution(6574867918882389764)
XLA Ops:
  0.6 2.6 %shard_map.84 = bf16[16,8,4,16,128]{4,3,2,1,0:T(8,128)(2,1)} custom-call(bf16[32,8192]{1,0:T(8,128)(2,1)} %q_hbm.1, bf16[32,8192]{1,0:T(8,128)(2,1)} %g_hbm.1, bf16[32,1024]{1,0:T(8,128)(2,1)} %k_hbm.1, bf16[32,1024]{1,0:T(8,128)(2,1)} %v_hbm.1), custom_call_target="tpu_custom_call" | custom-call | tf_op jit(solution)/shard_map/pallas_call | solution.py:373
  3.3 39.8 %all_to_all.10.got_ref = bf16[128,4,16,128]{3,2,1,0:T(8,128)(2,1)S(1)} all-to-all(bf16[128,4,16,128]{3,2,1,0:T(8,128)(2,1)} %bitcast.2), channel_id=1, replica_groups=mesh['ctx'=16,'tp'=8] {'ctx','tp'}, dimensions={0} | all-to-all | bytes 4194304 | tf_op jit(solution)/shard_map/all_to_all | solution.py:361
  43.1 0.0 copy-start
  43.1 0.1 shard_map.85.near_ref
  43.2 0.1 collective-permute-start
  43.3 0.5 copy-done
  43.8 0.2 convert_reduce_fusion
  44.0 0.1 pad_add_fusion.info_ref
  44.1 2.7 %shard_map.86 = (f32[10,512,512]{2,1,0:T(8,128)S(1)}, f32[4,8,512]{2,1,0:T(8,128)S(1)}, bf16[4,128,512]{2,1,0:T(8,128)(2,1)S(1)}, bf16[4,128,512]{2,1,0:T(8,128)(2,1)S(1)}) custom-call(s32[4]{0:T(128)S(1)} %pad_add_fusion.info_ref, bf16[128,4,16,128]{3,2,1,0:T(8,128)(2,1)S(1)} %all_to_all.10.got_ref, bf16[128,2,16,128]{3,2,1,0:T(8,128)(2,1)S(1)} %shard_map.85.near_ref), custom_call_target="tpu_custom_call" | custom-call | flops 4000000000 | bytes 1048576 | tf_op jit(solution)/shard_map/pallas_call | solution.py:410
  46.8 0.0 collective-permute-done.far_hbm
  46.8 12.0 %shard_map.87 = (bf16[128,16,128]{2,1,0:T(8,128)(2,1)S(1)}, f32[4,128,512]{2,1,0:T(8,128)S(1)}, f32[4,2,8,512]{3,2,1,0:T(8,128)S(1)}, bf16[128,2,16,128]{3,2,1,0:T(8,128)(2,1)S(1)}) custom-call(s32[4]{0:T(128)S(1)} %pad_add_fusion.info_ref, bf16[128,4,16,128]{3,2,1,0:T(8,128)(2,1)S(1)} %all_to_all.10.got_ref, ...), custom_call_target="tpu_custom_call" | custom-call | flops 16000000000 | bytes 1048576 | tf_op jit(solution)/shard_map/pallas_call | solution.py:422
  58.8 0.3 collective-permute-start.1
  59.0 5.2 %shard_map.88 = (bf16[128,16,128]{2,1,0:T(8,128)(2,1)S(1)}, f32[128,2,16,128]{3,2,1,0:T(8,128)S(1)}) custom-call(bf16[128,4,16,128]{3,2,1,0:T(8,128)(2,1)S(1)} %all_to_all.10.got_ref, bf16[128,2,16,128]{3,2,1,0:T(8,128)(2,1)S(1)} %shard_map.85.near_ref, f32[10,512,512]{2,1,0:T(8,128)S(1)} %get-tuple-element.14.s_near, ...), custom_call_target="tpu_custom_call" | custom-call | flops 8000000000 | bytes 1048576 | tf_op jit(solution)/shard_map/pallas_call | solution.py:447
  64.2 0.0 collective-permute-done.1.back_ref
  64.2 0.3 shard_map.89
  64.5 34.5 %all_to_all.11.got_ref = bf16[128,4,16,128]{3,2,1,0:T(8,128)(2,1)S(1)} all-to-all(bf16[128,4,16,128]{3,2,1,0:T(8,128)(2,1)S(1)} %shard_map.89), channel_id=1, replica_groups=mesh['ctx'=16,'tp'=8] {'ctx','tp'}, dimensions={0} | all-to-all | bytes 4194304 | tf_op jit(solution)/shard_map/all_to_all | solution.py:361
  99.1 1.5 %shard_map.90 = (f32[32,8192]{1,0:T(8,128)}, f32[32,8192]{1,0:T(8,128)}, f32[32,1024]{1,0:T(8,128)}, f32[32,1024]{1,0:T(8,128)}) custom-call(bf16[128,4,16,128]{3,2,1,0:T(8,128)(2,1)S(1)} %all_to_all.11.got_ref), custom_call_target="tpu_custom_call" | custom-call | tf_op jit(solution)/shard_map/pallas_call | solution.py:466
  (1 shorter events, 0.0 us)
Async XLA Ops:
  43.1 0.7 copy-start
  43.2 3.6 %collective-permute-start = (bf16[128,2,16,128]{3,2,1,0:T(8,128)(2,1)S(1)}, bf16[128,2,16,128]{3,2,1,0:T(8,128)(2,1)}, u32[]{:S(2)}, u32[]{:S(2)}) collective-permute-start(bf16[128,2,16,128]{3,2,1,0:T(8,128)(2,1)S(1)} %shard_map.85.near_ref), channel_id=1, source_target_pairs={{0,8},{8,0},{16,24},{24,16},{32,40},{40,32},{48,56},{56,48},{64,72... | collective-permute-start | bytes 3145736 | tf_op jit(solution)/shard_map/ppermute | solution.py:365
  58.8 5.4 %collective-permute-start.1 = (bf16[128,2,16,128]{3,2,1,0:T(8,128)(2,1)S(1)}, bf16[128,2,16,128]{3,2,1,0:T(8,128)(2,1)S(1)}, u32[]{:S(2)}, u32[]{:S(2)}) collective-permute-start(bf16[128,2,16,128]{3,2,1,0:T(8,128)(2,1)S(1)} %get-tuple-element.23), channel_id=1, source_target_pairs={{0,8},{8,0},{16,24},{24,16},{32,40},{40,32},{48,56},{56,48},{64,72... | collective-permute-start | bytes 3145736 | tf_op jit(solution)/shard_map/ppermute | solution.py:365

commit v5 on v4

--- a/solution.py
+++ b/solution.py
@@ -247,8 +247,8 @@
 
     run(scores(0) + scores(1))
     run(beside(mixes(0) + mixes(1), scores(2)))
-    run(beside(mixes(2), scores(3)))
-    run(beside(mixes(3), backs(0) + backs(1) + backs(2)))
+    run(beside(mixes(2), scores(3) + backs(0)))
+    run(beside(mixes(3), backs(1) + backs(2)))
     run(backs(3))
 
     def give(j, carry):

time: 102 us -> 102 us (level)
  no operation moved by 1% of the time
where the time goes in v5:
time: 102 us; the launch traced here: 101 us
  blocking collectives  74.4 us (73%)
  Pallas kernels  24.2 us (24%)
    all_to_all x2, blocking collectives, everyone(): return lax.all_to_all(x, ('ctx', 'tp'), 0, 0, tiled=True)  74.4 us
    pallas_call x1, Pallas kernels, per_device(): pl.pallas_call(far_kernel, out_shape=(out(single, bf16), out((BLOCKS, HD,...  11.8 us
    pallas_call x1, Pallas kernels, per_device(): pl.pallas_call(own_kernel, out_shape=(out(single, bf16), out(pair, f32)),...  5.16 us
    pallas_call x1, Pallas kernels, per_device(): pl.pallas_call(near_kernel, out_shape=(out((STEPS, FAR, ROWS), f32), out(...  2.66 us
    pallas_call x1, Pallas kernels, per_device(): pl.pallas_call(pack_kernel, out_shape=jax.ShapeDtypeStruct(packed, bf16),...  2.62 us
  transfers between devices with their start and end apart: 2, of which 0 were waited for; matrix products, arithmetic and copies ran while one was open for 0% of the time, Pallas kernels for 8%

profile of v5, /device:TPU:0, one launch (start us, length us, event | category | flops | bytes accessed | tf_op | source)
XLA Modules:
  0.0 100.7 jit_solution(1557421765625961430)
XLA Ops:
  0.6 2.6 %shard_map.84 = bf16[16,8,4,16,128]{4,3,2,1,0:T(8,128)(2,1)} custom-call(bf16[32,8192]{1,0:T(8,128)(2,1)} %q_hbm.1, bf16[32,8192]{1,0:T(8,128)(2,1)} %g_hbm.1, bf16[32,1024]{1,0:T(8,128)(2,1)} %k_hbm.1, bf16[32,1024]{1,0:T(8,128)(2,1)} %v_hbm.1), custom_call_target="tpu_custom_call" | custom-call | tf_op jit(solution)/shard_map/pallas_call | solution.py:373
  3.3 39.8 %all_to_all.10.got_ref = bf16[128,4,16,128]{3,2,1,0:T(8,128)(2,1)S(1)} all-to-all(bf16[128,4,16,128]{3,2,1,0:T(8,128)(2,1)} %bitcast.2), channel_id=1, replica_groups=mesh['ctx'=16,'tp'=8] {'ctx','tp'}, dimensions={0} | all-to-all | bytes 4194304 | tf_op jit(solution)/shard_map/all_to_all | solution.py:361
  43.1 0.0 copy-start
  43.1 0.1 shard_map.85.near_ref
  43.2 0.1 collective-permute-start
  43.3 0.5 copy-done
  43.8 0.2 convert_reduce_fusion
  44.0 0.1 pad_add_fusion.info_ref
  44.1 2.7 %shard_map.86 = (f32[10,512,512]{2,1,0:T(8,128)S(1)}, f32[4,8,512]{2,1,0:T(8,128)S(1)}, bf16[4,128,512]{2,1,0:T(8,128)(2,1)S(1)}, bf16[4,128,512]{2,1,0:T(8,128)(2,1)S(1)}) custom-call(s32[4]{0:T(128)S(1)} %pad_add_fusion.info_ref, bf16[128,4,16,128]{3,2,1,0:T(8,128)(2,1)S(1)} %all_to_all.10.got_ref, bf16[128,2,16,128]{3,2,1,0:T(8,128)(2,1)S(1)} %shard_map.85.near_ref), custom_call_target="tpu_custom_call" | custom-call | flops 4000000000 | bytes 1048576 | tf_op jit(solution)/shard_map/pallas_call | solution.py:410
  46.8 0.0 collective-permute-done.far_hbm
  46.8 11.8 %shard_map.87 = (bf16[128,16,128]{2,1,0:T(8,128)(2,1)S(1)}, f32[4,128,512]{2,1,0:T(8,128)S(1)}, f32[4,2,8,512]{3,2,1,0:T(8,128)S(1)}, bf16[128,2,16,128]{3,2,1,0:T(8,128)(2,1)S(1)}) custom-call(s32[4]{0:T(128)S(1)} %pad_add_fusion.info_ref, bf16[128,4,16,128]{3,2,1,0:T(8,128)(2,1)S(1)} %all_to_all.10.got_ref, ...), custom_call_target="tpu_custom_call" | custom-call | flops 16000000000 | bytes 1048576 | tf_op jit(solution)/shard_map/pallas_call | solution.py:422
  58.7 0.3 collective-permute-start.1
  58.9 5.2 %shard_map.88 = (bf16[128,16,128]{2,1,0:T(8,128)(2,1)S(1)}, f32[128,2,16,128]{3,2,1,0:T(8,128)S(1)}) custom-call(bf16[128,4,16,128]{3,2,1,0:T(8,128)(2,1)S(1)} %all_to_all.10.got_ref, bf16[128,2,16,128]{3,2,1,0:T(8,128)(2,1)S(1)} %shard_map.85.near_ref, f32[10,512,512]{2,1,0:T(8,128)S(1)} %get-tuple-element.14.s_near, ...), custom_call_target="tpu_custom_call" | custom-call | flops 8000000000 | bytes 1048576 | tf_op jit(solution)/shard_map/pallas_call | solution.py:447
  64.1 0.0 collective-permute-done.1.back_ref
  64.1 0.3 shard_map.89
  64.4 34.5 %all_to_all.11.got_ref = bf16[128,4,16,128]{3,2,1,0:T(8,128)(2,1)S(1)} all-to-all(bf16[128,4,16,128]{3,2,1,0:T(8,128)(2,1)S(1)} %shard_map.89), channel_id=1, replica_groups=mesh['ctx'=16,'tp'=8] {'ctx','tp'}, dimensions={0} | all-to-all | bytes 4194304 | tf_op jit(solution)/shard_map/all_to_all | solution.py:361
  99.0 1.5 %shard_map.90 = (f32[32,8192]{1,0:T(8,128)}, f32[32,8192]{1,0:T(8,128)}, f32[32,1024]{1,0:T(8,128)}, f32[32,1024]{1,0:T(8,128)}) custom-call(bf16[128,4,16,128]{3,2,1,0:T(8,128)(2,1)S(1)} %all_to_all.11.got_ref), custom_call_target="tpu_custom_call" | custom-call | tf_op jit(solution)/shard_map/pallas_call | solution.py:466
  (1 shorter events, 0.0 us)
Async XLA Ops:
  43.1 0.7 copy-start
  43.2 3.6 %collective-permute-start = (bf16[128,2,16,128]{3,2,1,0:T(8,128)(2,1)S(1)}, bf16[128,2,16,128]{3,2,1,0:T(8,128)(2,1)}, u32[]{:S(2)}, u32[]{:S(2)}) collective-permute-start(bf16[128,2,16,128]{3,2,1,0:T(8,128)(2,1)S(1)} %shard_map.85.near_ref), channel_id=1, source_target_pairs={{0,8},{8,0},{16,24},{24,16},{32,40},{40,32},{48,56},{56,48},{64,72... | collective-permute-start | bytes 3145736 | tf_op jit(solution)/shard_map/ppermute | solution.py:365
  58.7 5.4 %collective-permute-start.1 = (bf16[128,2,16,128]{3,2,1,0:T(8,128)(2,1)S(1)}, bf16[128,2,16,128]{3,2,1,0:T(8,128)(2,1)S(1)}, u32[]{:S(2)}, u32[]{:S(2)}) collective-permute-start(bf16[128,2,16,128]{3,2,1,0:T(8,128)(2,1)S(1)} %get-tuple-element.23), channel_id=1, source_target_pairs={{0,8},{8,0},{16,24},{24,16},{32,40},{40,32},{48,56},{56,48},{64,72... | collective-permute-start | bytes 3145736 | tf_op jit(solution)/shard_map/ppermute | solution.py:365
